TPU v7x, 32 devices: a whole 2x2x4 slice. The times are simulated.
32 devices in a mesh: view: 4 (over y, core), row: 8 (over z, x).
Axes of the slice: x: 2, y: 2, z: 4, core: 2. Of those that a mesh axis runs over, the one named last changes fastest.
Arguments:
- features: float32 [4, 16384, 2048], P('view', 'row'), may hold values from -0.125 to 0.125
- view_maps: float32 [4, 2048, 256], P('view', 'row'), may hold values from -6 to 6
- shared: float32 [16384, 256], P('row'), may hold values from -6 to 6
Outputs:
- maps_out: float32 [4, 2048, 256], P('view', 'row')
- shared_out: float32 [16384, 256], P('row')
All inputs are finite; a program needn't handle non-finite values.
Results may differ from a plain program's by a relative error of at most 0.00013.
Values sent between devices are 32-bit elements; how exact they have to be, the bound alone decides.
A program may use at most 128 MiB of HBM per device.

v0:
```python
import functools
import math

import jax
import jax.numpy as jnp
from jax import lax
from jax.experimental import pallas as pl
from jax.experimental.pallas import tpu as pltpu
from jax.sharding import PartitionSpec as P

ITERS = 2
NEWTON = 5
STEP_RATE = 0.5
CORES = 2
MESH = pl.DeviceIdType.MESH
F32 = jnp.float32
BF16 = jnp.bfloat16


def split(x):
    hi = x.astype(BF16)
    return hi, (x - hi.astype(F32)).astype(BF16)


def dot3s(a, b):
    lhs = jnp.concatenate([a[0], a[1], a[0]], axis=1)
    rhs = jnp.concatenate([b[0], b[0], b[1]], axis=0)
    return jnp.dot(lhs, rhs, preferred_element_type=F32)


def dot3(a, b):
    return dot3s(split(a), split(b))


def newton_root(gram):
    size = gram.shape[0]
    frob = jnp.sqrt(jnp.sum(gram * gram, keepdims=True))
    scaled = gram / frob
    rows = lax.broadcasted_iota(jnp.int32, (size, size), 0)
    cols = lax.broadcasted_iota(jnp.int32, (size, size), 1)
    eye = jnp.where(rows == cols, 1.0, 0.0).astype(F32)
    root = None
    for step in range(NEWTON):
        ym = split(scaled)
        zy = scaled if root is None else dot3s(split(root), ym)
        corr = 1.5 * eye - 0.5 * zy
        cs = split(corr)
        if step < NEWTON - 1:
            scaled = dot3s(ym, cs)
        root = corr if root is None else dot3s(cs, split(root))
    return root, frob


def kernel(
    dims,
    f_ref, w_ref, s_ref, wo_ref, so_ref,
    fhi, flo, fbuf, rthi, rtlo, y, wfull, gs, xr, zs, zr,
    vs, cr, yr, av, gram, gr, gv, gfull,
    f_sem, agz_s, agz_r, agx_s, agx_r, rsx_s, rsx_r, rsz_s, rsz_r,
    vrc_s, vrc_r, vry_s, vry_r, vgy_s, vgy_r, vgc_s, vgc_r,
    g1_s, g1_r, g2_s, g2_r, g3_s, g3_r,
):
    nz, nx, ny, nc = dims
    nrow, nview = nz * nx, ny * nc
    row, view = lax.axis_index("row"), lax.axis_index("view")
    z, x = row // nx, row % nx
    yy, core = view // nc, view % nc
    local = y.shape[0]
    width = f_ref.shape[2]
    keys = y.shape[1]
    shard = w_ref.shape[1]
    total = local * nrow
    step_size = STEP_RATE * width / total
    chunk = fbuf.shape[1]
    nchunk = local // chunk
    part = local // nview
    gpart = keys // nrow

    def at_row(zz, xx):
        return {"row": zz * nx + xx}

    def at_view(y1, c1):
        return {"view": y1 * nc + c1}

    def zmod(d):
        return lax.rem(z + d + nz, nz)

    def xmod(d):
        return lax.rem(x + d + nx, nx)

    def ymod(d):
        return lax.rem(yy + d + ny, ny)

    def cmod(d):
        return lax.rem(core + d + nc, nc)

    pending = []

    def send(src, dst, ssem, rsem, dev):
        copy = pltpu.make_async_remote_copy(
            src_ref=src, dst_ref=dst, send_sem=ssem, recv_sem=rsem,
            device_id=dev, device_id_type=MESH,
        )
        copy.start()
        pending.append(copy)

    def recv(buf, ssem, rsem, dev):
        pltpu.make_async_remote_copy(
            src_ref=buf, dst_ref=buf, send_sem=ssem, recv_sem=rsem,
            device_id=dev, device_id_type=MESH,
        ).wait_recv()

    def flush():
        for copy in pending:
            copy.wait_send()
        pending.clear()

    def load(c):
        return pltpu.make_async_copy(
            f_ref.at[0, pl.ds(c * chunk, chunk)], fbuf.at[c % 2], f_sem.at[c % 2]
        )

    load(0).start()
    wfull[0, row] = w_ref[0]
    barrier = pltpu.get_barrier_semaphore()
    for d in range(1, nrow):
        pl.semaphore_signal(
            barrier, inc=1, device_id={"row": lax.rem(row + d, nrow)}, device_id_type=MESH
        )
    for d in range(1, nview):
        pl.semaphore_signal(
            barrier, inc=1, device_id={"view": lax.rem(view + d, nview)}, device_id_type=MESH
        )
    pl.semaphore_wait(barrier, nrow + nview - 2)

    def gather_start(g):
        own = wfull.at[g, row]
        for dx in range(1, nx):
            send(own, own, agx_s.at[g, 0, dx], agx_r.at[g, 0, dx], at_row(z, xmod(dx)))
        for dz in range(1, nz):
            send(own, own, agz_s.at[g, dz], agz_r.at[g, dz], at_row(zmod(dz), x))

    def project(g, block, first):
        ws = split(wfull[g, block])
        rhs = jnp.concatenate([ws[0], ws[0], ws[1]], axis=0)

        @pl.loop(0, local // 512)
        def _(c):
            rows = pl.ds(pl.multiple_of(c * 512, 512), 512)
            hi, lo = fhi[block, rows], flo[block, rows]
            out = jnp.dot(
                jnp.concatenate([hi, lo, hi], axis=1), rhs, preferred_element_type=F32
            )
            if first:
                y[rows] = out
            else:
                y[rows] += out

    def gather_project(g):
        project(g, row, True)
        for dz in range(nz):
            zsrc = zmod(-dz)
            if dz:
                block = zsrc * nx + x
                got = wfull.at[g, block]
                recv(got, agz_s.at[g, dz], agz_r.at[g, dz], at_row(zsrc, x))
                for dx in range(1, nx):
                    send(
                        got, got, agx_s.at[g, dz, dx], agx_r.at[g, dz, dx],
                        at_row(z, xmod(dx)),
                    )
                project(g, block, False)
            prev = dz - 1
            if prev >= 0:
                x_part(g, prev)
        x_part(g, nz - 1)

    def x_part(g, dz):
        for dx in range(1, nx):
            xsrc = xmod(-dx)
            block = zmod(-dz) * nx + xsrc
            recv(
                wfull.at[g, block], agx_s.at[g, dz, dx], agx_r.at[g, dz, dx],
                at_row(z, xsrc),
            )
            project(g, block, False)

    def set_residual(shared_of):
        @pl.loop(0, local // 512)
        def _(c):
            rows = pl.ds(pl.multiple_of(c * 512, 512), 512)
            res = (y[rows] - shared_of(c, rows)).T
            hi, lo = split(res)
            rthi[:, rows] = hi
            rtlo[:, rows] = lo

    def gradient(block):
        hi, lo = fhi[block], flo[block]
        rh = rthi[...]
        out = jnp.dot(rh, hi, preferred_element_type=F32)
        out += jnp.dot(rh, lo, preferred_element_type=F32)
        out += jnp.dot(rtlo[...], hi, preferred_element_type=F32)
        return out

    def scatter_gradient(it):
        order = list(range(1, nz)) + [0]
        for dz in order:
            for dx in range(1, nx):
                xt = xmod(dx)
                gs[it, dz, dx] = gradient(zmod(dz) * nx + xt)
                send(
                    gs.at[it, dz, dx], xr.at[it, dz, dx],
                    rsx_s.at[it, dz, dx], rsx_r.at[it, dz, dx], at_row(z, xt),
                )
        acc = None
        for dz in order:
            zs[it, dz] = gradient(zmod(dz) * nx + x)
            for dx in range(1, nx):
                recv(
                    xr.at[it, dz, dx], rsx_s.at[it, dz, dx], rsx_r.at[it, dz, dx],
                    at_row(z, xmod(-dx)),
                )
                zs[it, dz] += xr[it, dz, dx]
            if dz:
                send(
                    zs.at[it, dz], zr.at[it, dz], rsz_s.at[it, dz], rsz_r.at[it, dz],
                    at_row(zmod(dz), x),
                )
        acc = zs[it, 0]
        for dz in range(1, nz):
            recv(
                zr.at[it, dz], rsz_s.at[it, dz], rsz_r.at[it, dz], at_row(zmod(-dz), x)
            )
            acc = acc + zr[it, dz]
        wfull[it + 1, row] = wfull[it, row] - step_size * acc.T

    def yblock(block):
        return pl.ds(pl.multiple_of(block * part, part), part)

    def view_average(it):
        order = list(range(1, ny)) + [0]
        for dy in order:
            for dc in range(1, nc):
                ct = cmod(dc)
                send(
                    y.at[yblock(ymod(dy) * nc + ct)], cr.at[it, dy, dc],
                    vrc_s.at[it, dy, dc], vrc_r.at[it, dy, dc], at_view(yy, ct),
                )
        for dy in order:
            acc = y[yblock(ymod(dy) * nc + core)]
            for dc in range(1, nc):
                recv(
                    cr.at[it, dy, dc], vrc_s.at[it, dy, dc], vrc_r.at[it, dy, dc],
                    at_view(yy, cmod(-dc)),
                )
                acc = acc + cr[it, dy, dc]
            vs[it, dy] = acc
            if dy:
                send(
                    vs.at[it, dy], yr.at[it, dy], vry_s.at[it, dy], vry_r.at[it, dy],
                    at_view(ymod(dy), core),
                )
        acc = vs[it, 0]
        for dy in range(1, ny):
            recv(
                yr.at[it, dy], vry_s.at[it, dy], vry_r.at[it, dy],
                at_view(ymod(-dy), core),
            )
            acc = acc + yr[it, dy]
        acc = acc / nview
        av[it, view] = acc
        own = av.at[it, view]
        for dy in range(1, ny):
            send(
                own, own, vgy_s.at[it, dy], vgy_r.at[it, dy], at_view(ymod(dy), core)
            )
        for dc in range(1, nc):
            send(
                own, own, vgc_s.at[it, 0, dc], vgc_r.at[it, 0, dc], at_view(yy, cmod(dc))
            )

    def reduce_gram(it):
        own = av[it, view]
        hi, lo = split(own)
        thi, tlo = split(own.T)
        gram[it] = dot3s((thi, tlo), (hi, lo)).reshape(nrow, gpart, keys)
        for d in range(1, nrow):
            to = lax.rem(row + d, nrow)
            send(
                gram.at[it, to], gr.at[it, d], g1_s.at[it, d], g1_r.at[it, d], {"row": to}
            )
        acc = gram[it, row]
        for d in range(1, nrow):
            recv(
                gr.at[it, d], g1_s.at[it, d], g1_r.at[it, d],
                {"row": lax.rem(row - d + nrow, nrow)},
            )
            acc = acc + gr[it, d]
        gv[it, 0] = acc
        for d in range(1, nview):
            send(
                gv.at[it, 0], gv.at[it, d], g2_s.at[it, d], g2_r.at[it, d],
                {"view": lax.rem(view + d, nview)},
            )
        acc = gv[it, 0]
        for d in range(1, nview):
            recv(
                gv.at[it, d], g2_s.at[it, d], g2_r.at[it, d],
                {"view": lax.rem(view - d + nview, nview)},
            )
            acc = acc + gv[it, d]
        gfull[it, row] = acc
        mine = gfull.at[it, row]
        for d in range(1, nrow):
            send(
                mine, mine, g3_s.at[it, d], g3_r.at[it, d],
                {"row": lax.rem(row + d, nrow)},
            )

    def forward_average(it):
        for dy in range(1, ny):
            ysrc = ymod(-dy)
            got = av.at[it, ysrc * nc + core]
            recv(got, vgy_s.at[it, dy], vgy_r.at[it, dy], at_view(ysrc, core))
            for dc in range(1, nc):
                send(
                    got, got, vgc_s.at[it, dy, dc], vgc_r.at[it, dy, dc],
                    at_view(yy, cmod(dc)),
                )

    def finish_average(it):
        for dy in range(ny):
            for dc in range(1, nc):
                csrc = cmod(-dc)
                recv(
                    av.at[it, ymod(-dy) * nc + csrc],
                    vgc_s.at[it, dy, dc], vgc_r.at[it, dy, dc], at_view(yy, csrc),
                )

    def finish_gram(it):
        for d in range(1, nrow):
            src = lax.rem(row - d + nrow, nrow)
            recv(gfull.at[it, src], g3_s.at[it, d], g3_r.at[it, d], {"row": src})
        return newton_root(gfull[it].reshape(keys, keys))

    gather_start(0)
    for c in range(nchunk):
        if c + 1 < nchunk:
            load(c + 1).start()
        load(c).wait()
        for b in range(nrow):
            hi, lo = split(fbuf[c % 2, :, b * shard:(b + 1) * shard])
            fhi[b, c * chunk:(c + 1) * chunk] = hi
            flo[b, c * chunk:(c + 1) * chunk] = lo
    gather_project(0)
    set_residual(lambda c, rows: s_ref[rows])
    for it in range(ITERS):
        scatter_gradient(it)
        gather_start(it + 1)
        gather_project(it + 1)
        view_average(it)
        reduce_gram(it)
        forward_average(it)
        root, frob = finish_gram(it)
        scale = jnp.sqrt(total / frob)
        finish_average(it)
        flush()
        rs = split(root)
        if it < ITERS - 1:
            for v in range(nview):
                rows = slice(v * part, (v + 1) * part)
                hi, lo = split((y[rows] - dot3s(split(av[it, v]), rs) * scale).T)
                rthi[:, rows] = hi
                rtlo[:, rows] = lo
        else:
            for v in range(nview):
                so_ref[v * part:(v + 1) * part] = dot3s(split(av[it, v]), rs) * scale
            wo_ref[0] = wfull[ITERS, row]


def solution(mesh):
    nrow, nview = mesh.shape["row"], mesh.shape["view"]
    nx = max(d for d in range(1, math.isqrt(nrow) + 1) if nrow % d == 0)
    nz = nrow // nx
    nc = CORES if nview % CORES == 0 else 1
    ny = nview // nc

    def local(features, view_maps, shared):
        rows, width = features.shape[1], features.shape[2]
        shard, keys = view_maps.shape[1], view_maps.shape[2]
        part, gpart = rows // nview, keys // nrow
        chunk = 256
        dma = pltpu.SemaphoreType.DMA
        sems = []
        for shape in [
            (ITERS + 1, nz), (ITERS + 1, nz, nx), (ITERS, nz, nx), (ITERS, nz),
            (ITERS, ny, nc), (ITERS, ny), (ITERS, ny), (ITERS, ny, nc),
            (ITERS, nrow), (ITERS, nview), (ITERS, nrow),
        ]:
            sems += [dma(shape), dma(shape)]
        vmem = pl.BlockSpec(memory_space=pltpu.VMEM)
        return pl.pallas_call(
            functools.partial(kernel, (nz, nx, ny, nc)),
            out_shape=(
                jax.ShapeDtypeStruct(view_maps.shape, F32),
                jax.ShapeDtypeStruct(shared.shape, F32),
            ),
            in_specs=[pl.BlockSpec(memory_space=pl.ANY), vmem, vmem],
            out_specs=(vmem, vmem),
            scratch_shapes=[
                pltpu.VMEM((nrow, rows, shard), BF16),
                pltpu.VMEM((nrow, rows, shard), BF16),
                pltpu.VMEM((2, chunk, width), F32),
                pltpu.VMEM((keys, rows), BF16),
                pltpu.VMEM((keys, rows), BF16),
                pltpu.VMEM((rows, keys), F32),
                pltpu.VMEM((ITERS + 1, nrow, shard, keys), F32),
                pltpu.VMEM((ITERS, nz, nx, keys, shard), F32),
                pltpu.VMEM((ITERS, nz, nx, keys, shard), F32),
                pltpu.VMEM((ITERS, nz, keys, shard), F32),
                pltpu.VMEM((ITERS, nz, keys, shard), F32),
                pltpu.VMEM((ITERS, ny, part, keys), F32),
                pltpu.VMEM((ITERS, ny, nc, part, keys), F32),
                pltpu.VMEM((ITERS, ny, part, keys), F32),
                pltpu.VMEM((ITERS, nview, part, keys), F32),
                pltpu.VMEM((ITERS, nrow, gpart, keys), F32),
                pltpu.VMEM((ITERS, nrow, gpart, keys), F32),
                pltpu.VMEM((ITERS, nview, gpart, keys), F32),
                pltpu.VMEM((ITERS, nrow, gpart, keys), F32),
                dma((2,)),
            ] + sems,
            compiler_params=pltpu.CompilerParams(
                collective_id=0, has_side_effects=True, vmem_limit_bytes=67043328
            ),
        )(features, view_maps, shared)

    in_specs = (P("view", "row", None), P("view", "row", None), P("row", None))
    out_specs = (P("view", "row", None), P("row", None))
    return jax.shard_map(local, mesh=mesh, in_specs=in_specs, out_specs=out_specs, check_vma=False)
```

profile of v0, /device:TPU:24, one launch (start us, length us, event | category | flops | bytes accessed | tf_op | source)
XLA Modules:
  0.0 260.7 jit_solution(4421589634857526854)
XLA Ops:
  0.6 255.3 %shard_map.50 = (f32[1,256,256]{2,1,0:T(8,128)}, f32[2048,256]{1,0:T(8,128)}) custom-call(f32[1,2048,2048]{2,1,0:T(8,128)} %f_ref.1, f32[1,256,256]{2,1,0:T(8,128)} %w_ref.1, f32[2048,256]{1,0:T(8,128)} %s_ref.1), custom_call_target="tpu_custom_call" | custom-call | tf_op jit(solution)/shard_map/pallas_call | solution.py:402
  255.9 1.7 copy.7
  257.6 3.0 %copy.8 = f32[2048,256]{1,0:T(8,128)} copy(f32[2048,256]{1,0:T(8,128)} %get-tuple-element.5) | data formatting | bytes 4194304
where the time goes:
time: 265 us; the launch traced here: 261 us
  Pallas kernels  255 us (96%)
  local copies, waits for them, and re-layouts  4.71 us (2%)
    pallas_call x1, Pallas kernels, local(): pl.pallas_call(functools.partial(kernel, (nz, nx, ny, nc)), out_shape=(ja...  255 us

commit v1 on v0

v1 whole, which is shorter than its diff:
```python
import functools
import math

import jax
import jax.numpy as jnp
from jax import lax
from jax.experimental import pallas as pl
from jax.experimental.pallas import tpu as pltpu
from jax.sharding import PartitionSpec as P

ITERS = 2
NEWTON = 5
STEP_RATE = 0.5
CORES = 2
LANES = 128
MESH = pl.DeviceIdType.MESH
F32 = jnp.float32
BF16 = jnp.bfloat16


def split(x):
    hi = x.astype(BF16)
    return hi, (x - hi.astype(F32)).astype(BF16)


def dot3s(a, b):
    lhs = jnp.concatenate([a[0], a[1], a[0]], axis=1)
    rhs = jnp.concatenate([b[0], b[0], b[1]], axis=0)
    return jnp.dot(lhs, rhs, preferred_element_type=F32)


def dot3(a, b):
    return dot3s(split(a), split(b))


def newton_steps(gram):
    size = gram.shape[0]
    frob = jnp.sqrt(jnp.sum(gram * gram, keepdims=True))
    scaled = gram / frob
    rows = lax.broadcasted_iota(jnp.int32, (size, size), 0)
    cols = lax.broadcasted_iota(jnp.int32, (size, size), 1)
    eye = jnp.where(rows == cols, 1.0, 0.0).astype(F32)
    root = None
    for step in range(NEWTON):
        ym = split(scaled)
        zy = scaled if root is None else dot3s(split(root), ym)
        corr = 1.5 * eye - 0.5 * zy
        cs = split(corr)
        if step < NEWTON - 1:
            scaled = dot3s(ym, cs)
        root = corr if root is None else dot3s(cs, split(root))
        yield root, frob


def kernel(
    dims,
    f_ref, w_ref, s_ref, wo_ref, so_ref,
    fhi, flo, fbuf, rthi, rtlo, y, wf, xs, xr, zs, zr,
    vs, cr, yr, av, gram, gr, gv, gfull,
    f_sem, agz_s, agz_r, agx_s, agx_r, rsx_s, rsx_r, rsz_s, rsz_r,
    vrc_s, vrc_r, vry_s, vry_r, vgy_s, vgy_r, vgc_s, vgc_r,
    g1_s, g1_r, g2_s, g2_r, g3_s, g3_r,
):
    nz, nx, ny, nc = dims
    nrow, nview = nz * nx, ny * nc
    row, view = lax.axis_index("row"), lax.axis_index("view")
    z, x = row // nx, row % nx
    yy, core = view // nc, view % nc
    local = y.shape[0]
    width = f_ref.shape[2]
    keys = y.shape[1]
    shard = w_ref.shape[1]
    total = local * nrow
    step_size = STEP_RATE * width / total
    chunk = fbuf.shape[1]
    nchunk = local // chunk
    part = local // nview
    gpart = keys // nrow
    cut, kp = wf.shape[2], wf.shape[4]
    sub = 512

    def at_row(zz, xx):
        return {"row": zz * nx + xx}

    def at_view(y1, c1):
        return {"view": y1 * nc + c1}

    def xmod(d):
        return lax.rem(x + d + nx, nx)

    def ymod(d):
        return lax.rem(yy + d + ny, ny)

    def cmod(d):
        return lax.rem(core + d + nc, nc)

    pending = []

    def remote(src, dst, ssem, rsem, dev):
        return pltpu.make_async_remote_copy(
            src_ref=src, dst_ref=dst, send_sem=ssem, recv_sem=rsem,
            device_id=dev, device_id_type=MESH,
        )

    def send(src, dst, ssem, rsem, dev):
        copy = remote(src, dst, ssem, rsem, dev)
        copy.start()
        pending.append(copy)

    def recv(buf, ssem, rsem, dev):
        remote(buf, buf, ssem, rsem, dev).wait_recv()

    def flush():
        for copy in pending:
            copy.wait_send()
        pending.clear()

    def line(j):
        low, high = z, nz - 1 - z
        m = jnp.minimum(low, high)
        near = j < 2 * m
        k = jnp.where(near, j // 2 + 1, j - m + 1)
        far_d = jnp.where(low > high, 1, -1)
        d = jnp.where(near, 1 - 2 * (j % 2), far_d)
        return z - d * k, d

    def inside(zz):
        return jnp.logical_and(zz >= 0, zz < nz)

    def load(c):
        return pltpu.make_async_copy(
            f_ref.at[0, pl.ds(c * chunk, chunk)], fbuf.at[c % 2], f_sem.at[c % 2]
        )

    load(0).start()
    for p in range(cut):
        wf[0, row, p] = w_ref[0, :, p * kp:(p + 1) * kp]
    barrier = pltpu.get_barrier_semaphore()
    for d in range(1, nrow):
        pl.semaphore_signal(
            barrier, inc=1, device_id={"row": lax.rem(row + d, nrow)}, device_id_type=MESH
        )
    for d in range(1, nview):
        pl.semaphore_signal(
            barrier, inc=1, device_id={"view": lax.rem(view + d, nview)}, device_id_type=MESH
        )
    pl.semaphore_wait(barrier, nrow + nview - 2)

    def ag_z(g, src, p, slot, to):
        ref = wf.at[g % 2, src * nx + x, p]
        return remote(ref, ref, agz_s.at[g, slot, p], agz_r.at[g, src, p], at_row(to, x))

    def ag_x(g, src, dx, p):
        ref = wf.at[g % 2, src * nx + x, p]
        return remote(
            ref, ref, agx_s.at[g, src, dx, p], agx_r.at[g, src, dx, p], at_row(z, xmod(dx))
        )

    def ag_own(g, p):
        @pl.when(z + 1 < nz)
        def _():
            ag_z(g, z, p, z, z + 1).start()

        @pl.when(z > 0)
        def _():
            ag_z(g, z, p, nz, z - 1).start()

        for dx in range(1, nx):
            ag_x(g, z, dx, p).start()

    def ag_event(g, j, p):
        src, d = line(j)
        ag_z(g, src, p, src, z - d).wait_recv()

        @pl.when(inside(z + d))
        def _():
            ag_z(g, src, p, src, z + d).start()

        for dx in range(1, nx):
            ag_x(g, src, dx, p).start()

    def ag_cross(g, src):
        for dx in range(1, nx):
            block = src * nx + xmod(-dx)
            for p in range(cut):
                recv(
                    wf.at[g % 2, block, p],
                    agx_s.at[g, src, dx, p], agx_r.at[g, src, dx, p], at_row(z, xmod(-dx)),
                )
            project(g, block, False)

    def ag_flush(g):
        for p in range(cut):
            @pl.when(z + 1 < nz)
            def _():
                ag_z(g, z, p, z, z + 1).wait_send()

            @pl.when(z > 0)
            def _():
                ag_z(g, z, p, nz, z - 1).wait_send()

            for dx in range(1, nx):
                ag_x(g, z, dx, p).wait_send()

        @pl.loop(0, nz - 1)
        def _(j):
            src, d = line(j)
            for p in range(cut):
                @pl.when(inside(z + d))
                def _():
                    ag_z(g, src, p, src, z + d).wait_send()

                for dx in range(1, nx):
                    ag_x(g, src, dx, p).wait_send()

    def project(g, block, first):
        wb = jnp.concatenate([wf[g % 2, block, p] for p in range(cut)], axis=1)
        ws = split(wb)
        rhs = jnp.concatenate([ws[0], ws[0], ws[1]], axis=0)

        @pl.loop(0, local // sub)
        def _(c):
            rows = pl.ds(pl.multiple_of(c * sub, sub), sub)
            hi, lo = fhi[block, rows], flo[block, rows]
            out = jnp.dot(
                jnp.concatenate([hi, lo, hi], axis=1), rhs, preferred_element_type=F32
            )
            if first:
                y[rows] = out
            else:
                y[rows] += out

    def ag_run(g, started):
        project(g, row, True)
        if not started:
            for p in range(cut):
                ag_event(g, 0, p)

        @pl.loop(0, nz - 1)
        def _(j):
            src, _ = line(j)
            project(g, src * nx + x, False)

            @pl.when(j + 1 < nz - 1)
            def _():
                for p in range(cut):
                    ag_event(g, j + 1, p)

            ag_cross(g, jnp.where(j == 0, z, line(j - 1)[0]))

        ag_cross(g, line(nz - 2)[0])

    def put_rt(rows, value):
        hi, lo = split(value.T)
        rthi[:, rows] = hi
        rtlo[:, rows] = lo

    def gradient(block):
        hi, lo = fhi[block], flo[block]
        rh = rthi[...]
        out = jnp.dot(rh, hi, preferred_element_type=F32)
        out += jnp.dot(rh, lo, preferred_element_type=F32)
        out += jnp.dot(rtlo[...], hi, preferred_element_type=F32)
        return out.reshape(cut, kp, shard)

    def order(i):
        return jnp.where(i == nz - 1, z, line(nz - 2 - i)[0])

    def rs_x(r, t, dx, p):
        return remote(
            xs.at[r % 2, t, dx - 1, p], xr.at[r % 2, t, dx - 1, p],
            rsx_s.at[r, t, dx, p], rsx_r.at[r, t, dx, p], at_row(z, xmod(dx)),
        )

    def rs_z(r, t, d, p):
        slot = jnp.where(jnp.logical_and(d < 0, t == z - d), nz, t)
        return remote(
            zs.at[r % 2, t, p], zr.at[r % 2, slot, p],
            rsz_s.at[r, t, p], rsz_r.at[r, slot, p], at_row(z - d, x),
        )

    def rs_compute(r):
        @pl.loop(0, nz)
        def _(i):
            t = order(i)
            for dx in range(1, nx):
                xs[r % 2, t, dx - 1] = gradient(t * nx + xmod(dx))
                for p in range(cut):
                    rs_x(r, t, dx, p).start()

        @pl.loop(0, nz)
        def _(i):
            t = order(i)
            zs[r % 2, t] = gradient(t * nx + x)

    def rs_over_x(r, t, p):
        acc = zs[r % 2, t, p]
        for dx in range(1, nx):
            recv(
                xr.at[r % 2, t, dx - 1, p],
                rsx_s.at[r, t, dx, p], rsx_r.at[r, t, dx, p], at_row(z, xmod(-dx)),
            )
            acc = acc + xr[r % 2, t, dx - 1, p]
        return acc

    def rs_take(r, t, slot, p, frm):
        recv(
            zr.at[r % 2, slot, p], rsz_s.at[r, t, p], rsz_r.at[r, slot, p], at_row(frm, x)
        )
        zs[r % 2, t, p] += zr[r % 2, slot, p]

    def rs_event(r, j, p):
        t, d = line(j)
        zs[r % 2, t, p] = rs_over_x(r, t, p)

        @pl.when(inside(z + d))
        def _():
            rs_take(r, t, t, p, z + d)

        rs_z(r, t, d, p).start()

    def rs_own(r, p):
        zs[r % 2, z, p] = rs_over_x(r, z, p)

        @pl.when(z + 1 < nz)
        def _():
            rs_take(r, z, z, p, z + 1)

        @pl.when(z > 0)
        def _():
            rs_take(r, z, nz, p, z - 1)

        return zs[r % 2, z, p]

    def rs_flush(r):
        @pl.loop(0, nz)
        def _(i):
            t = order(i)
            for dx in range(1, nx):
                for p in range(cut):
                    rs_x(r, t, dx, p).wait_send()

        @pl.loop(0, nz - 1)
        def _(j):
            t, d = line(j)
            for p in range(cut):
                rs_z(r, t, d, p).wait_send()

    def yblock(block):
        return pl.ds(pl.multiple_of(block * part, part), part)

    def view_send(it):
        for dy in list(range(1, ny)) + [0]:
            for dc in range(1, nc):
                ct = cmod(dc)
                send(
                    y.at[yblock(ymod(dy) * nc + ct)], cr.at[it, dy, dc - 1],
                    vrc_s.at[it, dy, dc], vrc_r.at[it, dy, dc], at_view(yy, ct),
                )

    def view_mid(it):
        for dy in list(range(1, ny)) + [0]:
            acc = y[yblock(ymod(dy) * nc + core)]
            for dc in range(1, nc):
                recv(
                    cr.at[it, dy, dc - 1], vrc_s.at[it, dy, dc], vrc_r.at[it, dy, dc],
                    at_view(yy, cmod(-dc)),
                )
                acc = acc + cr[it, dy, dc - 1]
            vs[it, dy] = acc
            if dy:
                send(
                    vs.at[it, dy], yr.at[it, dy], vry_s.at[it, dy], vry_r.at[it, dy],
                    at_view(ymod(dy), core),
                )

    def view_end(it):
        acc = vs[it, 0]
        for dy in range(1, ny):
            recv(
                yr.at[it, dy], vry_s.at[it, dy], vry_r.at[it, dy],
                at_view(ymod(-dy), core),
            )
            acc = acc + yr[it, dy]
        av[it, view] = acc / nview
        own = av.at[it, view]
        for dy in range(1, ny):
            send(
                own, own, vgy_s.at[it, dy], vgy_r.at[it, dy], at_view(ymod(dy), core)
            )
        for dc in range(1, nc):
            send(
                own, own, vgc_s.at[it, 0, dc], vgc_r.at[it, 0, dc], at_view(yy, cmod(dc))
            )

    def gram_start(it):
        own = av[it, view]
        hi, lo = split(own)
        thi, tlo = split(own.T)
        gram[it] = dot3s((thi, tlo), (hi, lo)).reshape(nrow, gpart, keys)
        for d in range(1, nrow):
            to = lax.rem(row + d, nrow)
            send(
                gram.at[it, to], gr.at[it, d], g1_s.at[it, d], g1_r.at[it, d], {"row": to}
            )

    def gram_views(it):
        acc = gram[it, row]
        for d in range(1, nrow):
            recv(
                gr.at[it, d], g1_s.at[it, d], g1_r.at[it, d],
                {"row": lax.rem(row - d + nrow, nrow)},
            )
            acc = acc + gr[it, d]
        gv[it, 0] = acc
        for d in range(1, nview):
            send(
                gv.at[it, 0], gv.at[it, d], g2_s.at[it, d], g2_r.at[it, d],
                {"view": lax.rem(view + d, nview)},
            )

    def gram_rows(it):
        acc = gv[it, 0]
        for d in range(1, nview):
            recv(
                gv.at[it, d], g2_s.at[it, d], g2_r.at[it, d],
                {"view": lax.rem(view - d + nview, nview)},
            )
            acc = acc + gv[it, d]
        gfull[it, row] = acc
        mine = gfull.at[it, row]
        for d in range(1, nrow):
            send(
                mine, mine, g3_s.at[it, d], g3_r.at[it, d],
                {"row": lax.rem(row + d, nrow)},
            )

    def gram_end(it):
        for d in range(1, nrow):
            src = lax.rem(row - d + nrow, nrow)
            recv(gfull.at[it, src], g3_s.at[it, d], g3_r.at[it, d], {"row": src})
        return newton_steps(gfull[it].reshape(keys, keys))

    def forward_average(it):
        for dy in range(1, ny):
            ysrc = ymod(-dy)
            got = av.at[it, ysrc * nc + core]
            recv(got, vgy_s.at[it, dy], vgy_r.at[it, dy], at_view(ysrc, core))
            for dc in range(1, nc):
                send(
                    got, got, vgc_s.at[it, dy, dc], vgc_r.at[it, dy, dc],
                    at_view(yy, cmod(dc)),
                )

    def finish_average(it):
        for dy in range(ny):
            for dc in range(1, nc):
                csrc = cmod(-dc)
                recv(
                    av.at[it, ymod(-dy) * nc + csrc],
                    vgc_s.at[it, dy, dc], vgc_r.at[it, dy, dc], at_view(yy, csrc),
                )

    far = nz - 2
    ns = jax.named_scope
    with ns("q_load"):
        for p in range(cut):
            ag_own(0, p)
        for c in range(nchunk):
            if c + 1 < nchunk:
                load(c + 1).start()
            load(c).wait()
            for b in range(nrow):
                hi, lo = split(fbuf[c % 2, :, b * shard:(b + 1) * shard])
                fhi[b, c * chunk:(c + 1) * chunk] = hi
                flo[b, c * chunk:(c + 1) * chunk] = lo
            if nchunk - c <= cut:
                ag_event(0, 0, cut - nchunk + c)
    with ns("q_ag0"):
        ag_run(0, True)
    with ns("q_res"):
        for c in range(local // sub):
            rows = slice(c * sub, (c + 1) * sub)
            put_rt(rows, y[rows] - s_ref[rows])
    with ns("q_rs0c"):
        rs_compute(0)
    with ns("q_rs0e"):
        @pl.loop(0, nz - 1)
        def _(i):
            for p in range(cut):
                rs_event(0, far - i, p)
        for p in range(cut):
            wf[1, row, p] = wf[0, row, p] - step_size * rs_own(0, p).T
            ag_own(1, p)
    with ns("q_fl"):
        ag_flush(0)
        rs_flush(0)
    with ns("q_ag1"):
        ag_run(1, False)
    with ns("q_vsend"):
        view_send(0)
        for c in range(local // sub):
            rows = slice(c * sub, (c + 1) * sub)
            put_rt(rows, y[rows])
    with ns("q_vmid"):
        view_mid(0)
    with ns("q_rs1c"):
        rs_compute(1)
    with ns("q_rs1e"):
        for p in range(cut):
            rs_event(1, far, p)
    with ns("q_vend"):
        view_end(0)
    with ns("q_g1"):
        gram_start(0)
    with ns("q_rs1e"):
        @pl.loop(1, nz - 1)
        def _(i):
            for p in range(cut):
                rs_event(1, far - i, p)
        for p in range(cut):
            rs_own(1, p)
    with ns("q_g2"):
        gram_views(0)
    with ns("q_fa"):
        forward_average(0)
    with ns("q_g3"):
        gram_rows(0)
    with ns("q_fin"):
        finish_average(0)
        ag_flush(1)
        rs_flush(1)
        for v in range(nview):
            put_rt(slice(v * part, (v + 1) * part), av[0, v])
    with ns("q_rs2c"):
        rs_compute(2)
    with ns("q_rs2e"):
        for p in range(cut):
            rs_event(2, far, p)
    with ns("q_nw"):
        steps = gram_end(0)
        next(steps)
        root, frob = next(steps)
    with ns("q_rs2e"):
        for i in range(1, nz - 1):
            for p in range(cut):
                rs_event(2, far - i, p)
            root, frob = next(steps, (root, frob))
        for root, frob in steps:
            pass
        for p in range(cut):
            rs_own(2, p)
    with ns("q_w2"):
        scale = jnp.sqrt(total / frob)
        moved = dot3s(split(zs[0, z].reshape(keys, shard).T), split(root)) * scale
        moved = step_size * (zs[1, z].reshape(keys, shard).T - moved)
        for p in range(cut):
            wf[0, row, p] = wf[1, row, p] - moved[:, p * kp:(p + 1) * kp]
            ag_own(2, p)
        flush()
        rs_flush(2)
    with ns("q_ag2"):
        ag_run(2, False)
    with ns("q_vmid"):
        view_send(1)
        view_mid(1)
        for p in range(cut):
            wo_ref[0, :, p * kp:(p + 1) * kp] = wf[0, row, p]
    with ns("q_vend"):
        view_end(1)
    with ns("q_g1"):
        gram_start(1)
        gram_views(1)
    with ns("q_g3"):
        gram_rows(1)
        ag_flush(2)
        forward_average(1)
    with ns("q_g4"):
        steps = gram_end(1)
    with ns("q_nw"):
        for root, frob in steps:
            pass
        scale = jnp.sqrt(total / frob)
    with ns("q_fina"):
        finish_average(1)
    with ns("q_out"):
        rs = split(root)
        for v in range(nview):
            so_ref[v * part:(v + 1) * part] = dot3s(split(av[1, v]), rs) * scale
        flush()


def solution(mesh):
    nrow, nview = mesh.shape["row"], mesh.shape["view"]
    nx = max(d for d in range(1, math.isqrt(nrow) + 1) if nrow % d == 0)
    nz = nrow // nx
    nc = CORES if nview % CORES == 0 else 1
    ny = nview // nc

    def local(features, view_maps, shared):
        rows, width = features.shape[1], features.shape[2]
        shard, keys = view_maps.shape[1], view_maps.shape[2]
        part, gpart = rows // nview, keys // nrow
        cut = max(1, keys // LANES)
        kp = keys // cut
        chunk = 256
        dma = pltpu.SemaphoreType.DMA
        sems = []
        for shape in [
            (3, nz + 1, cut), (3, nz, nx, cut), (3, nz, nx, cut), (3, nz + 1, cut),
            (ITERS, ny, nc), (ITERS, ny), (ITERS, ny), (ITERS, ny, nc),
            (ITERS, nrow), (ITERS, nview), (ITERS, nrow),
        ]:
            sems += [dma(shape), dma(shape)]
        vmem = pl.BlockSpec(memory_space=pltpu.VMEM)
        return pl.pallas_call(
            functools.partial(kernel, (nz, nx, ny, nc)),
            out_shape=(
                jax.ShapeDtypeStruct(view_maps.shape, F32),
                jax.ShapeDtypeStruct(shared.shape, F32),
            ),
            in_specs=[pl.BlockSpec(memory_space=pl.ANY), vmem, vmem],
            out_specs=(vmem, vmem),
            scratch_shapes=[
                pltpu.VMEM((nrow, rows, shard), BF16),
                pltpu.VMEM((nrow, rows, shard), BF16),
                pltpu.VMEM((2, chunk, width), F32),
                pltpu.VMEM((keys, rows), BF16),
                pltpu.VMEM((keys, rows), BF16),
                pltpu.VMEM((rows, keys), F32),
                pltpu.VMEM((2, nrow, cut, shard, kp), F32),
                pltpu.VMEM((2, nz, nx - 1, cut, kp, shard), F32),
                pltpu.VMEM((2, nz, nx - 1, cut, kp, shard), F32),
                pltpu.VMEM((2, nz, cut, kp, shard), F32),
                pltpu.VMEM((2, nz + 1, cut, kp, shard), F32),
                pltpu.VMEM((ITERS, ny, part, keys), F32),
                pltpu.VMEM((ITERS, ny, nc - 1, part, keys), F32),
                pltpu.VMEM((ITERS, ny, part, keys), F32),
                pltpu.VMEM((ITERS, nview, part, keys), F32),
                pltpu.VMEM((ITERS, nrow, gpart, keys), F32),
                pltpu.VMEM((ITERS, nrow, gpart, keys), F32),
                pltpu.VMEM((ITERS, nview, gpart, keys), F32),
                pltpu.VMEM((ITERS, nrow, gpart, keys), F32),
                dma((2,)),
            ] + sems,
            compiler_params=pltpu.CompilerParams(
                collective_id=0, has_side_effects=True, vmem_limit_bytes=67043328
            ),
        )(features, view_maps, shared)

    in_specs = (P("view", "row", None), P("view", "row", None), P("row", None))
    out_specs = (P("view", "row", None), P("row", None))
    return jax.shard_map(local, mesh=mesh, in_specs=in_specs, out_specs=out_specs, check_vma=False)
```

time: 265 us -> 231 us (0.87); the launches traced: 261 us -> 230 us
  Pallas kernels: 255 us -> 225 us
    pallas_call x1, Pallas kernels: 255 us -> 225 us  [local(): pl.pallas_call(functools.partial(kernel, (nz, nx, ny, nc)), out_shape=(ja...]
where the time goes in v1:
time: 231 us; the launch traced here: 230 us
  Pallas kernels  225 us (97%)
  local copies, waits for them, and re-layouts  4.71 us (2%)
    pallas_call x1, Pallas kernels, local(): pl.pallas_call(functools.partial(kernel, (nz, nx, ny, nc)), out_shape=(ja...  225 us
    unnamed x2, local copies, waits for them, and re-layouts  4.71 us

profile of v1, /device:TPU:24, one launch (start us, length us, event | category | flops | bytes accessed | tf_op | source)
XLA Modules:
  0.0 230.4 jit_solution(10031621397261034165)
XLA Ops:
  0.6 225.1 %shard_map.50 = (f32[1,256,256]{2,1,0:T(8,128)}, f32[2048,256]{1,0:T(8,128)}) custom-call(f32[1,2048,2048]{2,1,0:T(8,128)} %f_ref.1, f32[1,256,256]{2,1,0:T(8,128)} %w_ref.1, f32[2048,256]{1,0:T(8,128)} %s_ref.1), custom_call_target="tpu_custom_call" | custom-call | tf_op jit(solution)/shard_map/pallas_call | solution.py:616
  225.7 1.7 copy.7
  227.4 3.0 %copy.8 = f32[2048,256]{1,0:T(8,128)} copy(f32[2048,256]{1,0:T(8,128)} %get-tuple-element.5) | data formatting | bytes 4194304

commit v2 on v1

v2 whole, which is shorter than its diff:
```python
import functools
import math

import jax
import jax.numpy as jnp
from jax import lax
from jax.experimental import pallas as pl
from jax.experimental.pallas import tpu as pltpu
from jax.sharding import PartitionSpec as P

ITERS = 2
NEWTON = 5
STEP_RATE = 0.5
CORES = 2
SUBLANES = 8
HALVES = 2
CUT = 2
LATE = 0
MESH = pl.DeviceIdType.MESH
F32 = jnp.float32
BF16 = jnp.bfloat16


def split(x):
    hi = x.astype(BF16)
    return hi, (x - hi.astype(F32)).astype(BF16)


def dot3s(a, b):
    lhs = jnp.concatenate([a[0], a[1], a[0]], axis=1)
    rhs = jnp.concatenate([b[0], b[0], b[1]], axis=0)
    return jnp.dot(lhs, rhs, preferred_element_type=F32)


def dot3(a, b):
    return dot3s(split(a), split(b))


def newton_steps(gram):
    size = gram.shape[0]
    frob = jnp.sqrt(jnp.sum(gram * gram, keepdims=True))
    scaled = gram / frob
    rows = lax.broadcasted_iota(jnp.int32, (size, size), 0)
    cols = lax.broadcasted_iota(jnp.int32, (size, size), 1)
    eye = jnp.where(rows == cols, 1.0, 0.0).astype(F32)
    root = None
    for step in range(NEWTON):
        ym = split(scaled)
        zy = scaled if root is None else dot3s(split(root), ym)
        corr = 1.5 * eye - 0.5 * zy
        cs = split(corr)
        if step < NEWTON - 1:
            scaled = dot3s(ym, cs)
        root = corr if root is None else dot3s(cs, split(root))
        yield root, frob


def kernel(
    dims, pieces, cross,
    f_ref, w_ref, s_ref, wo_ref, so_ref,
    fhi, flo, fbuf, rthi, rtlo, y, wf, xs, xr, zs, zr, xq, zq,
    vs, cr, yr, av, gram, gr, gv, gfull,
    f_sem, agz_s, agz_r, agx_s, agx_r, rsx_s, rsx_r, rsz_s, rsz_r, rsq_s, rsq_r, rsxq_s, rsxq_r,
    vrc_s, vrc_r, vry_s, vry_r, vgy_s, vgy_r, vgc_s, vgc_r,
    g1_s, g1_r, g2_s, g2_r, g3_s, g3_r,
):
    nz, nx, ny, nc = dims
    nrow, nview = nz * nx, ny * nc
    row, view = lax.axis_index("row"), lax.axis_index("view")
    z, x = row // nx, row % nx
    yy, core = view // nc, view % nc
    local = y.shape[0]
    width = f_ref.shape[2]
    keys = y.shape[1]
    shard = w_ref.shape[1]
    total = local * nrow
    step_size = STEP_RATE * width / total
    chunk = fbuf.shape[1]
    nchunk = local // chunk
    part = local // nview
    gpart = keys // nrow
    cut = len(pieces)
    rows_of = [pl.ds(a, n) for a, n in pieces]
    crows = pl.ds(*cross)
    late = cross[1] > 0
    ends = range(cut + 1) if late else range(cut)
    rels = list(range(nx)) if late else []
    sub = 512

    def at_row(zz, xx):
        return {"row": zz * nx + xx}

    def at_view(y1, c1):
        return {"view": y1 * nc + c1}

    def xmod(d):
        return lax.rem(x + d + nx, nx)

    def ymod(d):
        return lax.rem(yy + d + ny, ny)

    def cmod(d):
        return lax.rem(core + d + nc, nc)

    pending = []

    def remote(src, dst, ssem, rsem, dev):
        return pltpu.make_async_remote_copy(
            src_ref=src, dst_ref=dst, send_sem=ssem, recv_sem=rsem,
            device_id=dev, device_id_type=MESH,
        )

    def send(src, dst, ssem, rsem, dev):
        copy = remote(src, dst, ssem, rsem, dev)
        copy.start()
        pending.append(copy)

    def recv(buf, ssem, rsem, dev):
        remote(buf, buf, ssem, rsem, dev).wait_recv()

    def flush():
        for copy in pending:
            copy.wait_send()
        pending.clear()

    def line(j):
        low, high = z, nz - 1 - z
        m = jnp.minimum(low, high)
        near = j < 2 * m
        k = jnp.where(near, j // 2 + 1, j - m + 1)
        far_d = jnp.where(low > high, 1, -1)
        d = jnp.where(near, 1 - 2 * (j % 2), far_d)
        return z - d * k, d

    def inside(zz):
        return jnp.logical_and(zz >= 0, zz < nz)

    def load(c):
        return pltpu.make_async_copy(
            f_ref.at[0, pl.ds(c * chunk, chunk)], fbuf.at[c % 2], f_sem.at[c % 2]
        )

    load(0).start()
    wf[0, row] = w_ref[0].T
    barrier = pltpu.get_barrier_semaphore()
    for d in range(1, nrow):
        pl.semaphore_signal(
            barrier, inc=1, device_id={"row": lax.rem(row + d, nrow)}, device_id_type=MESH
        )
    for d in range(1, nview):
        pl.semaphore_signal(
            barrier, inc=1, device_id={"view": lax.rem(view + d, nview)}, device_id_type=MESH
        )
    pl.semaphore_wait(barrier, nrow + nview - 2)

    def ag_z(g, src, p, rel, slot, to):
        rows = crows if p == cut else rows_of[p]
        ref = wf.at[g % 2, src * nx + xmod(rel), rows]
        return remote(
            ref, ref, agz_s.at[g, slot, p + rel], agz_r.at[g, src, p + rel], at_row(to, x)
        )

    def ag_x(g, src, dx, p):
        rows = crows if p == cut else rows_of[p]
        ref = wf.at[g % 2, src * nx + x, rows]
        return remote(
            ref, ref, agx_s.at[g, src, dx, p], agx_r.at[g, src, dx, p], at_row(z, xmod(dx))
        )

    def ag_both(g, p, rel, wait=False):
        @pl.when(z + 1 < nz)
        def _():
            copy = ag_z(g, z, p, rel, z, z + 1)
            copy.wait_send() if wait else copy.start()

        @pl.when(z > 0)
        def _():
            copy = ag_z(g, z, p, rel, nz, z - 1)
            copy.wait_send() if wait else copy.start()

    def ag_own(g, p):
        if p == cut:
            for dx in range(1, nx):
                ag_x(g, z, dx, p).start()
            ag_both(g, p, 0)
        else:
            ag_both(g, p, 0)
            for dx in range(1, nx):
                ag_x(g, z, dx, p).start()

    def ag_crossed(g):
        for dx in rels[1:]:
            recv(
                wf.at[g % 2, z * nx + xmod(-dx), crows],
                agx_s.at[g, z, dx, cut], agx_r.at[g, z, dx, cut], at_row(z, xmod(-dx)),
            )
            ag_both(g, cut, nx - dx)

    def ag_relay(g, j, p, rel, wait=False):
        src, d = line(j)
        if not wait:
            ag_z(g, src, p, rel, src, z - d).wait_recv()

        @pl.when(inside(z + d))
        def _():
            copy = ag_z(g, src, p, rel, src, z + d)
            copy.wait_send() if wait else copy.start()

    def ag_event(g, j, p):
        ag_relay(g, j, p, 0)
        for dx in range(1, nx):
            ag_x(g, line(j)[0], dx, p).start()

    def ag_last(g, src):
        for dx in range(1, nx):
            block = src * nx + xmod(-dx)
            for p in range(cut):
                recv(
                    wf.at[g % 2, block, rows_of[p]],
                    agx_s.at[g, src, dx, p], agx_r.at[g, src, dx, p], at_row(z, xmod(-dx)),
                )
            project(g, block, False)

    def ag_flush(g):
        for p in ends:
            ag_both(g, p, 0, True)
            for dx in range(1, nx):
                ag_x(g, z, dx, p).wait_send()
        for rel in rels[1:]:
            ag_both(g, cut, rel, True)

        @pl.loop(0, nz - 1)
        def _(j):
            for p in range(cut):
                ag_relay(g, j, p, 0, True)
                for dx in range(1, nx):
                    ag_x(g, line(j)[0], dx, p).wait_send()
            for rel in rels:
                ag_relay(g, j, cut, rel, True)

    def project(g, block, first):
        hi, lo = split(wf[g % 2, block])
        rhs = jnp.concatenate([hi, hi, lo], axis=1)

        @pl.loop(0, local // sub)
        def _(c):
            rows = pl.ds(pl.multiple_of(c * sub, sub), sub)
            fh, fl = fhi[block, rows], flo[block, rows]
            out = lax.dot_general(
                jnp.concatenate([fh, fl, fh], axis=1), rhs, (((1,), (1,)), ((), ())),
                preferred_element_type=F32,
            )
            if first:
                y[rows] = out
            else:
                y[rows] += out

    def ag_run(g, started):
        if not started:
            project(g, row, True)
            for p in range(cut):
                ag_event(g, 0, p)
            ag_crossed(g)
        else:
            project(g, row, True)

        @pl.loop(0, nz - 1)
        def _(j):
            @pl.when(j + 1 < nz - 1)
            def _():
                for p in range(cut):
                    ag_event(g, j + 1, p)

            for rel in rels:
                ag_relay(g, j, cut, rel)
            project(g, line(j)[0] * nx + x, False)
            ag_last(g, jnp.where(j == 0, z, line(j - 1)[0]))

        ag_last(g, line(nz - 2)[0])

    def put_rt(rows, value):
        hi, lo = split(value.T)
        rthi[:, rows] = hi
        rtlo[:, rows] = lo

    def gradient(block):
        hi, lo = fhi[block], flo[block]
        rh = rthi[...]
        out = jnp.dot(rh, hi, preferred_element_type=F32)
        out += jnp.dot(rh, lo, preferred_element_type=F32)
        out += jnp.dot(rtlo[...], hi, preferred_element_type=F32)
        return out

    def order(i):
        return jnp.where(i == nz - 1, z, line(nz - 2 - i)[0])

    def rs_x(r, t, dx, p):
        return remote(
            xs.at[r % 2, t, dx - 1, rows_of[p]], xr.at[r % 2, t, dx - 1, rows_of[p]],
            rsx_s.at[r, t, dx, p], rsx_r.at[r, t, dx, p], at_row(z, xmod(dx)),
        )

    def slot_of(t, d):
        return jnp.where(jnp.logical_and(d < 0, t == z - d), nz, t)

    def rs_z(r, t, d, p):
        slot = slot_of(t, d)
        return remote(
            zs.at[r % 2, t, rows_of[p]], zr.at[r % 2, slot, rows_of[p]],
            rsz_s.at[r, t, p], rsz_r.at[r, slot, p], at_row(z - d, x),
        )

    def mine(r, t, rel):
        return zs.at[r % 2, t, crows] if rel == 0 else xs.at[r % 2, t, rel - 1, crows]

    def rs_q(r, t, d, rel):
        slot = slot_of(t, d)
        return remote(
            mine(r, t, rel), zq.at[r % 2, slot, rel],
            rsq_s.at[r, t, rel], rsq_r.at[r, slot, rel], at_row(z - d, x),
        )

    def rs_qx(r, rel):
        return remote(
            mine(r, z, rel), xq.at[r % 2, rel - 1],
            rsxq_s.at[r, rel], rsxq_r.at[r, rel], at_row(z, xmod(rel)),
        )

    def rs_first(r, i):
        t = order(i)
        for dx in range(1, nx):
            xs[r % 2, t, dx - 1] = gradient(t * nx + xmod(dx))
            for p in range(cut):
                rs_x(r, t, dx, p).start()

    def rs_compute(r, begun=0):
        @pl.loop(begun, nz)
        def _(i):
            rs_first(r, i)

        @pl.loop(0, nz)
        def _(i):
            t = order(i)
            zs[r % 2, t] = gradient(t * nx + x)

    def rs_over_x(r, t, p):
        acc = zs[r % 2, t, rows_of[p]]
        for dx in range(1, nx):
            recv(
                xr.at[r % 2, t, dx - 1, rows_of[p]],
                rsx_s.at[r, t, dx, p], rsx_r.at[r, t, dx, p], at_row(z, xmod(-dx)),
            )
            acc = acc + xr[r % 2, t, dx - 1, rows_of[p]]
        return acc

    def rs_take(r, t, slot, p, frm):
        recv(
            zr.at[r % 2, slot, rows_of[p]], rsz_s.at[r, t, p], rsz_r.at[r, slot, p],
            at_row(frm, x),
        )
        zs[r % 2, t, rows_of[p]] += zr[r % 2, slot, rows_of[p]]

    def rs_qtake(r, t, slot, rel, frm):
        recv(
            zq.at[r % 2, slot, rel], rsq_s.at[r, t, rel], rsq_r.at[r, slot, rel],
            at_row(frm, x),
        )
        mine(r, t, rel)[...] += zq[r % 2, slot, rel]

    def rs_event(r, j):
        t, d = line(j)
        for rel in rels:
            @pl.when(inside(z + d))
            def _():
                rs_qtake(r, t, t, rel, z + d)

            rs_q(r, t, d, rel).start()
        for p in range(cut):
            zs[r % 2, t, rows_of[p]] = rs_over_x(r, t, p)

            @pl.when(inside(z + d))
            def _():
                rs_take(r, t, t, p, z + d)

            rs_z(r, t, d, p).start()

    def rs_cross(r):
        for rel in rels[1:] + rels[:1]:
            @pl.when(z + 1 < nz)
            def _():
                rs_qtake(r, z, z, rel, z + 1)

            @pl.when(z > 0)
            def _():
                rs_qtake(r, z, nz, rel, z - 1)

            if rel:
                rs_qx(r, rel).start()

    def rs_own(r, p):
        if p == cut:
            acc = zs[r % 2, z, crows]
            for dx in range(1, nx):
                recv(
                    xq.at[r % 2, dx - 1], rsxq_s.at[r, dx], rsxq_r.at[r, dx],
                    at_row(z, xmod(-dx)),
                )
                acc = acc + xq[r % 2, dx - 1]
            zs[r % 2, z, crows] = acc
            return acc
        zs[r % 2, z, rows_of[p]] = rs_over_x(r, z, p)

        @pl.when(z + 1 < nz)
        def _():
            rs_take(r, z, z, p, z + 1)

        @pl.when(z > 0)
        def _():
            rs_take(r, z, nz, p, z - 1)

        return zs[r % 2, z, rows_of[p]]

    def rs_flush(r):
        @pl.loop(0, nz)
        def _(i):
            t = order(i)
            for dx in range(1, nx):
                for p in range(cut):
                    rs_x(r, t, dx, p).wait_send()

        @pl.loop(0, nz - 1)
        def _(j):
            t, d = line(j)
            for p in range(cut):
                rs_z(r, t, d, p).wait_send()
            for rel in rels:
                rs_q(r, t, d, rel).wait_send()

        for rel in rels[1:]:
            rs_qx(r, rel).wait_send()

    half = part // HALVES
    halves = [pl.ds(h * half, half) for h in range(HALVES)]

    def yblock(block, h):
        return pl.ds(pl.multiple_of(block * part + h * half, half), half)

    def view_send(it):
        for dy in list(range(1, ny)) + [0]:
            for h in range(HALVES):
                for dc in range(1, nc):
                    ct = cmod(dc)
                    send(
                        y.at[yblock(ymod(dy) * nc + ct, h)], cr.at[it, dy, dc - 1, halves[h]],
                        vrc_s.at[it, dy, dc, h], vrc_r.at[it, dy, dc, h], at_view(yy, ct),
                    )

    def view_mid(it):
        for dy in list(range(1, ny)) + [0]:
            for h in range(HALVES):
                acc = y[yblock(ymod(dy) * nc + core, h)]
                for dc in range(1, nc):
                    recv(
                        cr.at[it, dy, dc - 1, halves[h]],
                        vrc_s.at[it, dy, dc, h], vrc_r.at[it, dy, dc, h],
                        at_view(yy, cmod(-dc)),
                    )
                    acc = acc + cr[it, dy, dc - 1, halves[h]]
                vs[it, dy, halves[h]] = acc
                if dy:
                    send(
                        vs.at[it, dy, halves[h]], yr.at[it, dy, halves[h]],
                        vry_s.at[it, dy, h], vry_r.at[it, dy, h], at_view(ymod(dy), core),
                    )

    def view_end(it, h):
        acc = vs[it, 0, halves[h]]
        for dy in range(1, ny):
            recv(
                yr.at[it, dy, halves[h]], vry_s.at[it, dy, h], vry_r.at[it, dy, h],
                at_view(ymod(-dy), core),
            )
            acc = acc + yr[it, dy, halves[h]]
        av[it, view, halves[h]] = acc / nview
        own = av.at[it, view, halves[h]]
        for dy in range(1, ny):
            send(
                own, own, vgy_s.at[it, dy, h], vgy_r.at[it, dy, h], at_view(ymod(dy), core)
            )
        for dc in range(1, nc):
            send(
                own, own, vgc_s.at[it, 0, dc, h], vgc_r.at[it, 0, dc, h],
                at_view(yy, cmod(dc)),
            )

    def gram_start(it):
        own = av[it, view]
        hi, lo = split(own)
        thi, tlo = split(own.T)
        gram[it] = dot3s((thi, tlo), (hi, lo)).reshape(nrow, gpart, keys)
        for d in range(1, nrow):
            to = lax.rem(row + d, nrow)
            send(
                gram.at[it, to], gr.at[it, d], g1_s.at[it, d], g1_r.at[it, d], {"row": to}
            )

    def gram_views(it):
        acc = gram[it, row]
        for d in range(1, nrow):
            recv(
                gr.at[it, d], g1_s.at[it, d], g1_r.at[it, d],
                {"row": lax.rem(row - d + nrow, nrow)},
            )
            acc = acc + gr[it, d]
        gv[it, 0] = acc
        for d in range(1, nview):
            send(
                gv.at[it, 0], gv.at[it, d], g2_s.at[it, d], g2_r.at[it, d],
                {"view": lax.rem(view + d, nview)},
            )

    def gram_rows(it):
        acc = gv[it, 0]
        for d in range(1, nview):
            recv(
                gv.at[it, d], g2_s.at[it, d], g2_r.at[it, d],
                {"view": lax.rem(view - d + nview, nview)},
            )
            acc = acc + gv[it, d]
        gfull[it, row] = acc
        mine = gfull.at[it, row]
        for d in range(1, nrow):
            send(
                mine, mine, g3_s.at[it, d], g3_r.at[it, d],
                {"row": lax.rem(row + d, nrow)},
            )

    def gram_end(it):
        for d in range(1, nrow):
            src = lax.rem(row - d + nrow, nrow)
            recv(gfull.at[it, src], g3_s.at[it, d], g3_r.at[it, d], {"row": src})
        return newton_steps(gfull[it].reshape(keys, keys))

    def forward_average(it, h):
        for dy in range(1, ny):
            ysrc = ymod(-dy)
            got = av.at[it, ysrc * nc + core, halves[h]]
            recv(got, vgy_s.at[it, dy, h], vgy_r.at[it, dy, h], at_view(ysrc, core))
            for dc in range(1, nc):
                send(
                    got, got, vgc_s.at[it, dy, dc, h], vgc_r.at[it, dy, dc, h],
                    at_view(yy, cmod(dc)),
                )

    def finish_average(it):
        for dy in range(ny):
            for h in range(HALVES):
                for dc in range(1, nc):
                    csrc = cmod(-dc)
                    recv(
                        av.at[it, ymod(-dy) * nc + csrc, halves[h]],
                        vgc_s.at[it, dy, dc, h], vgc_r.at[it, dy, dc, h], at_view(yy, csrc),
                    )

    far = nz - 2
    ns = jax.named_scope
    with ns("q_load"):
        for p in list(ends[cut:]) + list(range(cut)):
            ag_own(0, p)
        for c in range(nchunk):
            if c + 1 < nchunk:
                load(c + 1).start()
            load(c).wait()
            for b in range(nrow):
                hi, lo = split(fbuf[c % 2, :, b * shard:(b + 1) * shard])
                fhi[b, c * chunk:(c + 1) * chunk] = hi
                flo[b, c * chunk:(c + 1) * chunk] = lo
            if nchunk - c == cut + 1:
                ag_crossed(0)
            if nchunk - c <= cut:
                ag_event(0, 0, cut - nchunk + c)
    with ns("q_ag0"):
        ag_run(0, True)
    with ns("q_res"):
        for c in range(local // sub):
            rows = slice(c * sub, (c + 1) * sub)
            put_rt(rows, y[rows] - s_ref[rows])
    with ns("q_rs0c"):
        rs_compute(0)
    with ns("q_rs0e"):
        @pl.loop(0, nz - 1)
        def _(i):
            rs_event(0, far - i)
        rs_cross(0)
        for p in ends:
            rows = crows if p == cut else rows_of[p]
            wf[1, row, rows] = wf[0, row, rows] - step_size * rs_own(0, p)
            ag_own(1, p)
    with ns("q_fl"):
        ag_flush(0)
        rs_flush(0)
    with ns("q_ag1"):
        ag_run(1, False)
    with ns("q_vsend"):
        view_send(0)
        for c in range(local // sub):
            rows = slice(c * sub, (c + 1) * sub)
            put_rt(rows, y[rows])
        rs_first(1, 0)
    with ns("q_vmid"):
        view_mid(0)
    with ns("q_rs1c"):
        rs_compute(1, 1)
    with ns("q_rs1e"):
        rs_event(1, far)
    with ns("q_vend"):
        for h in range(HALVES):
            view_end(0, h)
    with ns("q_g1"):
        gram_start(0)
    with ns("q_rs1e"):
        @pl.loop(1, nz - 1)
        def _(i):
            rs_event(1, far - i)
    with ns("q_fa"):
        for h in range(HALVES - 1):
            forward_average(0, h)
    with ns("q_g2"):
        gram_views(0)
    with ns("q_fa"):
        forward_average(0, HALVES - 1)
    with ns("q_g3"):
        gram_rows(0)
    with ns("q_fin"):
        rs_cross(1)
        finish_average(0)
        ag_flush(1)
        for v in range(nview):
            put_rt(slice(v * part, (v + 1) * part), av[0, v])
    with ns("q_rs2c"):
        rs_compute(2)
    with ns("q_rs1o"):
        for p in ends:
            rs_own(1, p)
    with ns("q_rs2e"):
        rs_event(2, far)
    with ns("q_nw"):
        steps = gram_end(0)
        next(steps)
        root, frob = next(steps)
    with ns("q_rs2e"):
        for i in range(1, nz - 1):
            rs_event(2, far - i)
            root, frob = next(steps, (root, frob))
        for root, frob in steps:
            pass
        rs_cross(2)
        rootc = split(root.T)
        scale = jnp.sqrt(total / frob)
        for p in ends:
            rs_own(2, p)
    with ns("q_w2"):
        moved = dot3s(rootc, split(zs[0, z])) * scale
        wf[0, row] = wf[1, row] - step_size * (zs[1, z] - moved)
        for p in ends:
            ag_own(2, p)
        flush()
        rs_flush(1)
        rs_flush(2)
    with ns("q_ag2"):
        ag_run(2, False)
    with ns("q_vmid"):
        view_send(1)
        view_mid(1)
        wo_ref[0] = wf[0, row].T
    with ns("q_vend"):
        for h in range(HALVES):
            view_end(1, h)
    with ns("q_g1"):
        gram_start(1)
        gram_views(1)
    with ns("q_g3"):
        gram_rows(1)
        ag_flush(2)
        for h in range(HALVES):
            forward_average(1, h)
    with ns("q_g4"):
        steps = gram_end(1)
    with ns("q_nw"):
        for root, frob in steps:
            pass
        scale = jnp.sqrt(total / frob)
    with ns("q_fina"):
        finish_average(1)
    with ns("q_out"):
        rs = split(root)
        for v in range(nview):
            so_ref[v * part:(v + 1) * part] = dot3s(split(av[1, v]), rs) * scale
        flush()


def solution(mesh):
    nrow, nview = mesh.shape["row"], mesh.shape["view"]
    nx = max(d for d in range(1, math.isqrt(nrow) + 1) if nrow % d == 0)
    nz = nrow // nx
    nc = CORES if nview % CORES == 0 else 1
    ny = nview // nc

    def local(features, view_maps, shared):
        rows, width = features.shape[1], features.shape[2]
        shard, keys = view_maps.shape[1], view_maps.shape[2]
        part, gpart = rows // nview, keys // nrow
        tiles = keys // SUBLANES
        late = tiles * LATE // 32
        sizes = [(tiles - late + CUT - 1 - p) // CUT * SUBLANES for p in range(CUT)]
        pieces = [(sum(sizes[:p]), sizes[p]) for p in range(CUT)]
        cross = (sum(sizes), keys - sum(sizes))
        cut = CUT
        chunk = 256
        dma = pltpu.SemaphoreType.DMA
        sems = []
        for shape in [
            (3, nz + 1, cut + nx), (3, nz, nx, cut + 1), (3, nz, nx, cut), (3, nz + 1, cut),
            (3, nz + 1, nx), (3, nx),
            (ITERS, ny, nc, HALVES), (ITERS, ny, HALVES), (ITERS, ny, HALVES),
            (ITERS, ny, nc, HALVES),
            (ITERS, nrow), (ITERS, nview), (ITERS, nrow),
        ]:
            sems += [dma(shape), dma(shape)]
        vmem = pl.BlockSpec(memory_space=pltpu.VMEM)
        return pl.pallas_call(
            functools.partial(kernel, (nz, nx, ny, nc), pieces, cross),
            out_shape=(
                jax.ShapeDtypeStruct(view_maps.shape, F32),
                jax.ShapeDtypeStruct(shared.shape, F32),
            ),
            in_specs=[pl.BlockSpec(memory_space=pl.ANY), vmem, vmem],
            out_specs=(vmem, vmem),
            scratch_shapes=[
                pltpu.VMEM((nrow, rows, shard), BF16),
                pltpu.VMEM((nrow, rows, shard), BF16),
                pltpu.VMEM((2, chunk, width), F32),
                pltpu.VMEM((keys, rows), BF16),
                pltpu.VMEM((keys, rows), BF16),
                pltpu.VMEM((rows, keys), F32),
                pltpu.VMEM((2, nrow, keys, shard), F32),
                pltpu.VMEM((2, nz, nx - 1, keys, shard), F32),
                pltpu.VMEM((2, nz, nx - 1, keys, shard), F32),
                pltpu.VMEM((2, nz, keys, shard), F32),
                pltpu.VMEM((2, nz + 1, keys, shard), F32),
                pltpu.VMEM((2, nx - 1, max(cross[1], 8), shard), F32),
                pltpu.VMEM((2, nz + 1, nx, max(cross[1], 8), shard), F32),
                pltpu.VMEM((ITERS, ny, part, keys), F32),
                pltpu.VMEM((ITERS, ny, nc - 1, part, keys), F32),
                pltpu.VMEM((ITERS, ny, part, keys), F32),
                pltpu.VMEM((ITERS, nview, part, keys), F32),
                pltpu.VMEM((ITERS, nrow, gpart, keys), F32),
                pltpu.VMEM((ITERS, nrow, gpart, keys), F32),
                pltpu.VMEM((ITERS, nview, gpart, keys), F32),
                pltpu.VMEM((ITERS, nrow, gpart, keys), F32),
                dma((2,)),
            ] + sems,
            compiler_params=pltpu.CompilerParams(
                collective_id=0, has_side_effects=True, vmem_limit_bytes=67043328
            ),
        )(features, view_maps, shared)

    in_specs = (P("view", "row", None), P("view", "row", None), P("row", None))
    out_specs = (P("view", "row", None), P("row", None))
    return jax.shard_map(local, mesh=mesh, in_specs=in_specs, out_specs=out_specs, check_vma=False)
```

time: 231 us -> 226 us (0.978)
  Pallas kernels: 225 us -> 220 us
    pallas_call x1, Pallas kernels: 225 us -> 220 us  [local(): pl.pallas_call(functools.partial(kernel, (nz, nx, ny, nc), pieces, cross)...]
where the time goes in v2:
time: 226 us; the launch traced here: 225 us
  Pallas kernels  220 us (97%)
  local copies, waits for them, and re-layouts  4.71 us (2%)
    pallas_call x1, Pallas kernels, local(): pl.pallas_call(functools.partial(kernel, (nz, nx, ny, nc), pieces, cross)...  220 us
    unnamed x2, local copies, waits for them, and re-layouts  4.71 us

profile of v2, /device:TPU:24, one launch (start us, length us, event | category | flops | bytes accessed | tf_op | source)
XLA Modules:
  0.0 225.4 jit_solution(7575063554168945982)
XLA Ops:
  0.6 220.1 %shard_map.50 = (f32[1,256,256]{2,1,0:T(8,128)}, f32[2048,256]{1,0:T(8,128)}) custom-call(f32[1,2048,2048]{2,1,0:T(8,128)} %f_ref.1, f32[1,256,256]{2,1,0:T(8,128)} %w_ref.1, f32[2048,256]{1,0:T(8,128)} %s_ref.1), custom_call_target="tpu_custom_call" | custom-call | tf_op jit(solution)/shard_map/pallas_call | solution.py:731
  220.7 1.7 copy.7
  222.4 3.0 %copy.8 = f32[2048,256]{1,0:T(8,128)} copy(f32[2048,256]{1,0:T(8,128)} %get-tuple-element.5) | data formatting | bytes 4194304

commit v3 on v2

--- a/solution.py
+++ b/solution.py
@@ -12,10 +12,8 @@
 NEWTON = 5
 STEP_RATE = 0.5
 CORES = 2
-SUBLANES = 8
 HALVES = 2
 CUT = 2
-LATE = 0
 MESH = pl.DeviceIdType.MESH
 F32 = jnp.float32
 BF16 = jnp.bfloat16
@@ -56,11 +54,11 @@
 
 
 def kernel(
-    dims, pieces, cross,
-    f_ref, w_ref, s_ref, wo_ref, so_ref,
-    fhi, flo, fbuf, rthi, rtlo, y, wf, xs, xr, zs, zr, xq, zq,
+    dims, pieces,
+    f_ref, w_ref, s_hbm, wo_ref, ao_hbm, root_ref,
+    s_ref, fhi, flo, fbuf, rthi, rtlo, y, wf, xs, xr, zs, zr,
     vs, cr, yr, av, gram, gr, gv, gfull,
-    f_sem, agz_s, agz_r, agx_s, agx_r, rsx_s, rsx_r, rsz_s, rsz_r, rsq_s, rsq_r, rsxq_s, rsxq_r,
+    f_sem, s_sem, o_sem, agz_s, agz_r, agx_s, agx_r, rsx_s, rsx_r, rsz_s, rsz_r,
     vrc_s, vrc_r, vry_s, vry_r, vgy_s, vgy_r, vgc_s, vgc_r,
     g1_s, g1_r, g2_s, g2_r, g3_s, g3_r,
 ):
@@ -81,10 +79,6 @@
     gpart = keys // nrow
     cut = len(pieces)
     rows_of = [pl.ds(a, n) for a, n in pieces]
-    crows = pl.ds(*cross)
-    late = cross[1] > 0
-    ends = range(cut + 1) if late else range(cut)
-    rels = list(range(nx)) if late else []
     sub = 512
 
     def at_row(zz, xx):
@@ -141,6 +135,7 @@
         )
 
     load(0).start()
+    shared_load = pltpu.make_async_copy(s_hbm, s_ref, s_sem)
     wf[0, row] = w_ref[0].T
     barrier = pltpu.get_barrier_semaphore()
     for d in range(1, nrow):
@@ -153,61 +148,44 @@
         )
     pl.semaphore_wait(barrier, nrow + nview - 2)
 
-    def ag_z(g, src, p, rel, slot, to):
-        rows = crows if p == cut else rows_of[p]
-        ref = wf.at[g % 2, src * nx + xmod(rel), rows]
+    def ag_z(g, src, p, slot, to):
+        ref = wf.at[g % 2, src * nx + x, rows_of[p]]
+        return remote(ref, ref, agz_s.at[slot, p], agz_r.at[src, p], at_row(to, x))
+
+    def ag_x(g, src, dx, p):
+        ref = wf.at[g % 2, src * nx + x, rows_of[p]]
         return remote(
-            ref, ref, agz_s.at[g, slot, p + rel], agz_r.at[g, src, p + rel], at_row(to, x)
-        )
-
-    def ag_x(g, src, dx, p):
-        rows = crows if p == cut else rows_of[p]
-        ref = wf.at[g % 2, src * nx + x, rows]
-        return remote(
-            ref, ref, agx_s.at[g, src, dx, p], agx_r.at[g, src, dx, p], at_row(z, xmod(dx))
-        )
-
-    def ag_both(g, p, rel, wait=False):
+            ref, ref, agx_s.at[src, dx - 1, p], agx_r.at[src, dx - 1, p], at_row(z, xmod(dx))
+        )
+
+    def ag_both(g, p, wait=False):
         @pl.when(z + 1 < nz)
         def _():
-            copy = ag_z(g, z, p, rel, z, z + 1)
+            copy = ag_z(g, z, p, z, z + 1)
             copy.wait_send() if wait else copy.start()
 
         @pl.when(z > 0)
         def _():
-            copy = ag_z(g, z, p, rel, nz, z - 1)
+            copy = ag_z(g, z, p, nz, z - 1)
             copy.wait_send() if wait else copy.start()
 
     def ag_own(g, p):
-        if p == cut:
-            for dx in range(1, nx):
-                ag_x(g, z, dx, p).start()
-            ag_both(g, p, 0)
-        else:
-            ag_both(g, p, 0)
-            for dx in range(1, nx):
-                ag_x(g, z, dx, p).start()
-
-    def ag_crossed(g):
-        for dx in rels[1:]:
-            recv(
-                wf.at[g % 2, z * nx + xmod(-dx), crows],
-                agx_s.at[g, z, dx, cut], agx_r.at[g, z, dx, cut], at_row(z, xmod(-dx)),
-            )
-            ag_both(g, cut, nx - dx)
-
-    def ag_relay(g, j, p, rel, wait=False):
+        ag_both(g, p)
+        for dx in range(1, nx):
+            ag_x(g, z, dx, p).start()
+
+    def ag_relay(g, j, p, wait=False):
         src, d = line(j)
         if not wait:
-            ag_z(g, src, p, rel, src, z - d).wait_recv()
+            ag_z(g, src, p, src, z - d).wait_recv()
 
         @pl.when(inside(z + d))
         def _():
-            copy = ag_z(g, src, p, rel, src, z + d)
+            copy = ag_z(g, src, p, src, z + d)
             copy.wait_send() if wait else copy.start()
 
     def ag_event(g, j, p):
-        ag_relay(g, j, p, 0)
+        ag_relay(g, j, p)
         for dx in range(1, nx):
             ag_x(g, line(j)[0], dx, p).start()
 
@@ -217,26 +195,22 @@
             for p in range(cut):
                 recv(
                     wf.at[g % 2, block, rows_of[p]],
-                    agx_s.at[g, src, dx, p], agx_r.at[g, src, dx, p], at_row(z, xmod(-dx)),
+                    agx_s.at[src, dx - 1, p], agx_r.at[src, dx - 1, p], at_row(z, xmod(-dx)),
                 )
             project(g, block, False)
 
     def ag_flush(g):
-        for p in ends:
-            ag_both(g, p, 0, True)
+        for p in range(cut):
+            ag_both(g, p, True)
             for dx in range(1, nx):
                 ag_x(g, z, dx, p).wait_send()
-        for rel in rels[1:]:
-            ag_both(g, cut, rel, True)
 
         @pl.loop(0, nz - 1)
         def _(j):
             for p in range(cut):
-                ag_relay(g, j, p, 0, True)
+                ag_relay(g, j, p, True)
                 for dx in range(1, nx):
                     ag_x(g, line(j)[0], dx, p).wait_send()
-            for rel in rels:
-                ag_relay(g, j, cut, rel, True)
 
     def project(g, block, first):
         hi, lo = split(wf[g % 2, block])
@@ -256,13 +230,10 @@
                 y[rows] += out
 
     def ag_run(g, started):
+        project(g, row, True)
         if not started:
-            project(g, row, True)
             for p in range(cut):
                 ag_event(g, 0, p)
-            ag_crossed(g)
-        else:
-            project(g, row, True)
 
         @pl.loop(0, nz - 1)
         def _(j):
@@ -271,8 +242,6 @@
                 for p in range(cut):
                     ag_event(g, j + 1, p)
 
-            for rel in rels:
-                ag_relay(g, j, cut, rel)
             project(g, line(j)[0] * nx + x, False)
             ag_last(g, jnp.where(j == 0, z, line(j - 1)[0]))
 
@@ -297,7 +266,7 @@
     def rs_x(r, t, dx, p):
         return remote(
             xs.at[r % 2, t, dx - 1, rows_of[p]], xr.at[r % 2, t, dx - 1, rows_of[p]],
-            rsx_s.at[r, t, dx, p], rsx_r.at[r, t, dx, p], at_row(z, xmod(dx)),
+            rsx_s.at[r % 2, t, dx - 1, p], rsx_r.at[r % 2, t, dx - 1, p], at_row(z, xmod(dx)),
         )
 
     def slot_of(t, d):
@@ -307,23 +276,7 @@
         slot = slot_of(t, d)
         return remote(
             zs.at[r % 2, t, rows_of[p]], zr.at[r % 2, slot, rows_of[p]],
-            rsz_s.at[r, t, p], rsz_r.at[r, slot, p], at_row(z - d, x),
-        )
-
-    def mine(r, t, rel):
-        return zs.at[r % 2, t, crows] if rel == 0 else xs.at[r % 2, t, rel - 1, crows]
-
-    def rs_q(r, t, d, rel):
-        slot = slot_of(t, d)
-        return remote(
-            mine(r, t, rel), zq.at[r % 2, slot, rel],
-            rsq_s.at[r, t, rel], rsq_r.at[r, slot, rel], at_row(z - d, x),
-        )
-
-    def rs_qx(r, rel):
-        return remote(
-            mine(r, z, rel), xq.at[r % 2, rel - 1],
-            rsxq_s.at[r, rel], rsxq_r.at[r, rel], at_row(z, xmod(rel)),
+            rsz_s.at[r % 2, t, p], rsz_r.at[r % 2, slot, p], at_row(z - d, x),
         )
 
     def rs_first(r, i):
@@ -348,33 +301,20 @@
         for dx in range(1, nx):
             recv(
                 xr.at[r % 2, t, dx - 1, rows_of[p]],
-                rsx_s.at[r, t, dx, p], rsx_r.at[r, t, dx, p], at_row(z, xmod(-dx)),
+                rsx_s.at[r % 2, t, dx - 1, p], rsx_r.at[r % 2, t, dx - 1, p], at_row(z, xmod(-dx)),
             )
             acc = acc + xr[r % 2, t, dx - 1, rows_of[p]]
         return acc
 
     def rs_take(r, t, slot, p, frm):
         recv(
-            zr.at[r % 2, slot, rows_of[p]], rsz_s.at[r, t, p], rsz_r.at[r, slot, p],
+            zr.at[r % 2, slot, rows_of[p]], rsz_s.at[r % 2, t, p], rsz_r.at[r % 2, slot, p],
             at_row(frm, x),
         )
         zs[r % 2, t, rows_of[p]] += zr[r % 2, slot, rows_of[p]]
-
-    def rs_qtake(r, t, slot, rel, frm):
-        recv(
-            zq.at[r % 2, slot, rel], rsq_s.at[r, t, rel], rsq_r.at[r, slot, rel],
-            at_row(frm, x),
-        )
-        mine(r, t, rel)[...] += zq[r % 2, slot, rel]
 
     def rs_event(r, j):
         t, d = line(j)
-        for rel in rels:
-            @pl.when(inside(z + d))
-            def _():
-                rs_qtake(r, t, t, rel, z + d)
-
-            rs_q(r, t, d, rel).start()
         for p in range(cut):
             zs[r % 2, t, rows_of[p]] = rs_over_x(r, t, p)
 
@@ -384,30 +324,7 @@
 
             rs_z(r, t, d, p).start()
 
-    def rs_cross(r):
-        for rel in rels[1:] + rels[:1]:
-            @pl.when(z + 1 < nz)
-            def _():
-                rs_qtake(r, z, z, rel, z + 1)
-
-            @pl.when(z > 0)
-            def _():
-                rs_qtake(r, z, nz, rel, z - 1)
-
-            if rel:
-                rs_qx(r, rel).start()
-
     def rs_own(r, p):
-        if p == cut:
-            acc = zs[r % 2, z, crows]
-            for dx in range(1, nx):
-                recv(
-                    xq.at[r % 2, dx - 1], rsxq_s.at[r, dx], rsxq_r.at[r, dx],
-                    at_row(z, xmod(-dx)),
-                )
-                acc = acc + xq[r % 2, dx - 1]
-            zs[r % 2, z, crows] = acc
-            return acc
         zs[r % 2, z, rows_of[p]] = rs_over_x(r, z, p)
 
         @pl.when(z + 1 < nz)
@@ -433,11 +350,6 @@
             t, d = line(j)
             for p in range(cut):
                 rs_z(r, t, d, p).wait_send()
-            for rel in rels:
-                rs_q(r, t, d, rel).wait_send()
-
-        for rel in rels[1:]:
-            rs_qx(r, rel).wait_send()
 
     half = part // HALVES
     halves = [pl.ds(h * half, half) for h in range(HALVES)]
@@ -452,7 +364,7 @@
                     ct = cmod(dc)
                     send(
                         y.at[yblock(ymod(dy) * nc + ct, h)], cr.at[it, dy, dc - 1, halves[h]],
-                        vrc_s.at[it, dy, dc, h], vrc_r.at[it, dy, dc, h], at_view(yy, ct),
+                        vrc_s.at[dy, dc - 1, h], vrc_r.at[dy, dc - 1, h], at_view(yy, ct),
                     )
 
     def view_mid(it):
@@ -462,7 +374,7 @@
                 for dc in range(1, nc):
                     recv(
                         cr.at[it, dy, dc - 1, halves[h]],
-                        vrc_s.at[it, dy, dc, h], vrc_r.at[it, dy, dc, h],
+                        vrc_s.at[dy, dc - 1, h], vrc_r.at[dy, dc - 1, h],
                         at_view(yy, cmod(-dc)),
                     )
                     acc = acc + cr[it, dy, dc - 1, halves[h]]
@@ -470,14 +382,14 @@
                 if dy:
                     send(
                         vs.at[it, dy, halves[h]], yr.at[it, dy, halves[h]],
-                        vry_s.at[it, dy, h], vry_r.at[it, dy, h], at_view(ymod(dy), core),
+                        vry_s.at[dy - 1, h], vry_r.at[dy - 1, h], at_view(ymod(dy), core),
                     )
 
     def view_end(it, h):
         acc = vs[it, 0, halves[h]]
         for dy in range(1, ny):
             recv(
-                yr.at[it, dy, halves[h]], vry_s.at[it, dy, h], vry_r.at[it, dy, h],
+                yr.at[it, dy, halves[h]], vry_s.at[dy - 1, h], vry_r.at[dy - 1, h],
                 at_view(ymod(-dy), core),
             )
             acc = acc + yr[it, dy, halves[h]]
@@ -485,11 +397,11 @@
         own = av.at[it, view, halves[h]]
         for dy in range(1, ny):
             send(
-                own, own, vgy_s.at[it, dy, h], vgy_r.at[it, dy, h], at_view(ymod(dy), core)
+                own, own, vgy_s.at[dy - 1, h], vgy_r.at[dy - 1, h], at_view(ymod(dy), core)
             )
         for dc in range(1, nc):
             send(
-                own, own, vgc_s.at[it, 0, dc, h], vgc_r.at[it, 0, dc, h],
+                own, own, vgc_s.at[0, dc - 1, h], vgc_r.at[0, dc - 1, h],
                 at_view(yy, cmod(dc)),
             )
 
@@ -501,21 +413,21 @@
         for d in range(1, nrow):
             to = lax.rem(row + d, nrow)
             send(
-                gram.at[it, to], gr.at[it, d], g1_s.at[it, d], g1_r.at[it, d], {"row": to}
+                gram.at[it, to], gr.at[it, d], g1_s.at[d - 1], g1_r.at[d - 1], {"row": to}
             )
 
     def gram_views(it):
         acc = gram[it, row]
         for d in range(1, nrow):
             recv(
-                gr.at[it, d], g1_s.at[it, d], g1_r.at[it, d],
+                gr.at[it, d], g1_s.at[d - 1], g1_r.at[d - 1],
                 {"row": lax.rem(row - d + nrow, nrow)},
             )
             acc = acc + gr[it, d]
         gv[it, 0] = acc
         for d in range(1, nview):
             send(
-                gv.at[it, 0], gv.at[it, d], g2_s.at[it, d], g2_r.at[it, d],
+                gv.at[it, 0], gv.at[it, d], g2_s.at[d - 1], g2_r.at[d - 1],
                 {"view": lax.rem(view + d, nview)},
             )
 
@@ -523,7 +435,7 @@
         acc = gv[it, 0]
         for d in range(1, nview):
             recv(
-                gv.at[it, d], g2_s.at[it, d], g2_r.at[it, d],
+                gv.at[it, d], g2_s.at[d - 1], g2_r.at[d - 1],
                 {"view": lax.rem(view - d + nview, nview)},
             )
             acc = acc + gv[it, d]
@@ -531,24 +443,24 @@
         mine = gfull.at[it, row]
         for d in range(1, nrow):
             send(
-                mine, mine, g3_s.at[it, d], g3_r.at[it, d],
+                mine, mine, g3_s.at[d - 1], g3_r.at[d - 1],
                 {"row": lax.rem(row + d, nrow)},
             )
 
     def gram_end(it):
         for d in range(1, nrow):
             src = lax.rem(row - d + nrow, nrow)
-            recv(gfull.at[it, src], g3_s.at[it, d], g3_r.at[it, d], {"row": src})
+            recv(gfull.at[it, src], g3_s.at[d - 1], g3_r.at[d - 1], {"row": src})
         return newton_steps(gfull[it].reshape(keys, keys))
 
     def forward_average(it, h):
         for dy in range(1, ny):
             ysrc = ymod(-dy)
             got = av.at[it, ysrc * nc + core, halves[h]]
-            recv(got, vgy_s.at[it, dy, h], vgy_r.at[it, dy, h], at_view(ysrc, core))
+            recv(got, vgy_s.at[dy - 1, h], vgy_r.at[dy - 1, h], at_view(ysrc, core))
             for dc in range(1, nc):
                 send(
-                    got, got, vgc_s.at[it, dy, dc, h], vgc_r.at[it, dy, dc, h],
+                    got, got, vgc_s.at[dy, dc - 1, h], vgc_r.at[dy, dc - 1, h],
                     at_view(yy, cmod(dc)),
                 )
 
@@ -559,29 +471,30 @@
                     csrc = cmod(-dc)
                     recv(
                         av.at[it, ymod(-dy) * nc + csrc, halves[h]],
-                        vgc_s.at[it, dy, dc, h], vgc_r.at[it, dy, dc, h], at_view(yy, csrc),
+                        vgc_s.at[dy, dc - 1, h], vgc_r.at[dy, dc - 1, h], at_view(yy, csrc),
                     )
 
     far = nz - 2
     ns = jax.named_scope
     with ns("q_load"):
-        for p in list(ends[cut:]) + list(range(cut)):
+        for p in range(cut):
             ag_own(0, p)
         for c in range(nchunk):
             if c + 1 < nchunk:
                 load(c + 1).start()
+            else:
+                shared_load.start()
             load(c).wait()
             for b in range(nrow):
                 hi, lo = split(fbuf[c % 2, :, b * shard:(b + 1) * shard])
                 fhi[b, c * chunk:(c + 1) * chunk] = hi
                 flo[b, c * chunk:(c + 1) * chunk] = lo
-            if nchunk - c == cut + 1:
-                ag_crossed(0)
             if nchunk - c <= cut:
                 ag_event(0, 0, cut - nchunk + c)
     with ns("q_ag0"):
         ag_run(0, True)
     with ns("q_res"):
+        shared_load.wait()
         for c in range(local // sub):
             rows = slice(c * sub, (c + 1) * sub)
             put_rt(rows, y[rows] - s_ref[rows])
@@ -591,13 +504,12 @@
         @pl.loop(0, nz - 1)
         def _(i):
             rs_event(0, far - i)
-        rs_cross(0)
-        for p in ends:
-            rows = crows if p == cut else rows_of[p]
+        ag_flush(0)
+        for p in range(cut):
+            rows = rows_of[p]
             wf[1, row, rows] = wf[0, row, rows] - step_size * rs_own(0, p)
             ag_own(1, p)
     with ns("q_fl"):
-        ag_flush(0)
         rs_flush(0)
     with ns("q_ag1"):
         ag_run(1, False)
@@ -632,7 +544,6 @@
     with ns("q_g3"):
         gram_rows(0)
     with ns("q_fin"):
-        rs_cross(1)
         finish_average(0)
         ag_flush(1)
         for v in range(nview):
@@ -640,7 +551,7 @@
     with ns("q_rs2c"):
         rs_compute(2)
     with ns("q_rs1o"):
-        for p in ends:
+        for p in range(cut):
             rs_own(1, p)
     with ns("q_rs2e"):
         rs_event(2, far)
@@ -654,15 +565,14 @@
             root, frob = next(steps, (root, frob))
         for root, frob in steps:
             pass
-        rs_cross(2)
         rootc = split(root.T)
         scale = jnp.sqrt(total / frob)
-        for p in ends:
+        for p in range(cut):
             rs_own(2, p)
     with ns("q_w2"):
         moved = dot3s(rootc, split(zs[0, z])) * scale
         wf[0, row] = wf[1, row] - step_size * (zs[1, z] - moved)
-        for p in ends:
+        for p in range(cut):
             ag_own(2, p)
         flush()
         rs_flush(1)
@@ -684,19 +594,26 @@
         ag_flush(2)
         for h in range(HALVES):
             forward_average(1, h)
+        finish_average(1)
+        out = pltpu.make_async_copy(av.at[1], ao_hbm, o_sem)
+        out.start()
     with ns("q_g4"):
         steps = gram_end(1)
     with ns("q_nw"):
         for root, frob in steps:
             pass
-        scale = jnp.sqrt(total / frob)
-    with ns("q_fina"):
-        finish_average(1)
+        root_ref[...] = root * jnp.sqrt(total / frob)
     with ns("q_out"):
-        rs = split(root)
-        for v in range(nview):
-            so_ref[v * part:(v + 1) * part] = dot3s(split(av[1, v]), rs) * scale
+        out.wait()
         flush()
+
+
+def last_product(w_ref, a_ref, root_ref, wo_ref, so_ref):
+    @pl.when(pl.program_id(0) == 0)
+    def _():
+        wo_ref[...] = w_ref[...]
+
+    so_ref[...] = dot3(a_ref[...], root_ref[...])
 
 
 def solution(mesh):
@@ -710,33 +627,30 @@
         rows, width = features.shape[1], features.shape[2]
         shard, keys = view_maps.shape[1], view_maps.shape[2]
         part, gpart = rows // nview, keys // nrow
-        tiles = keys // SUBLANES
-        late = tiles * LATE // 32
-        sizes = [(tiles - late + CUT - 1 - p) // CUT * SUBLANES for p in range(CUT)]
-        pieces = [(sum(sizes[:p]), sizes[p]) for p in range(CUT)]
-        cross = (sum(sizes), keys - sum(sizes))
         cut = CUT
+        pieces = [(p * keys // cut, keys // cut) for p in range(cut)]
         chunk = 256
         dma = pltpu.SemaphoreType.DMA
         sems = []
         for shape in [
-            (3, nz + 1, cut + nx), (3, nz, nx, cut + 1), (3, nz, nx, cut), (3, nz + 1, cut),
-            (3, nz + 1, nx), (3, nx),
-            (ITERS, ny, nc, HALVES), (ITERS, ny, HALVES), (ITERS, ny, HALVES),
-            (ITERS, ny, nc, HALVES),
-            (ITERS, nrow), (ITERS, nview), (ITERS, nrow),
+            (nz + 1, cut), (nz, nx - 1, cut), (2, nz, nx - 1, cut), (2, nz + 1, cut),
+            (ny, nc - 1, HALVES), (ny - 1, HALVES), (ny - 1, HALVES), (ny, nc - 1, HALVES),
+            (nrow - 1,), (nview - 1,), (nrow - 1,),
         ]:
             sems += [dma(shape), dma(shape)]
         vmem = pl.BlockSpec(memory_space=pltpu.VMEM)
-        return pl.pallas_call(
-            functools.partial(kernel, (nz, nx, ny, nc), pieces, cross),
+        hbm = pl.BlockSpec(memory_space=pl.ANY)
+        maps, average, root = pl.pallas_call(
+            functools.partial(kernel, (nz, nx, ny, nc), pieces),
             out_shape=(
                 jax.ShapeDtypeStruct(view_maps.shape, F32),
-                jax.ShapeDtypeStruct(shared.shape, F32),
+                jax.ShapeDtypeStruct((nview, part, keys), F32),
+                jax.ShapeDtypeStruct((keys, keys), F32),
             ),
-            in_specs=[pl.BlockSpec(memory_space=pl.ANY), vmem, vmem],
-            out_specs=(vmem, vmem),
+            in_specs=[hbm, vmem, hbm],
+            out_specs=(vmem, hbm, vmem),
             scratch_shapes=[
+                pltpu.VMEM((rows, keys), F32),
                 pltpu.VMEM((nrow, rows, shard), BF16),
                 pltpu.VMEM((nrow, rows, shard), BF16),
                 pltpu.VMEM((2, chunk, width), F32),
@@ -748,8 +662,6 @@
                 pltpu.VMEM((2, nz, nx - 1, keys, shard), F32),
                 pltpu.VMEM((2, nz, keys, shard), F32),
                 pltpu.VMEM((2, nz + 1, keys, shard), F32),
-                pltpu.VMEM((2, nx - 1, max(cross[1], 8), shard), F32),
-                pltpu.VMEM((2, nz + 1, nx, max(cross[1], 8), shard), F32),
                 pltpu.VMEM((ITERS, ny, part, keys), F32),
                 pltpu.VMEM((ITERS, ny, nc - 1, part, keys), F32),
                 pltpu.VMEM((ITERS, ny, part, keys), F32),
@@ -758,12 +670,24 @@
                 pltpu.VMEM((ITERS, nrow, gpart, keys), F32),
                 pltpu.VMEM((ITERS, nview, gpart, keys), F32),
                 pltpu.VMEM((ITERS, nrow, gpart, keys), F32),
-                dma((2,)),
+                dma((2,)), dma, dma,
             ] + sems,
             compiler_params=pltpu.CompilerParams(
                 collective_id=0, has_side_effects=True, vmem_limit_bytes=67043328
             ),
         )(features, view_maps, shared)
+        whole = pl.BlockSpec((1, shard, keys), lambda c: (0, 0, 0))
+        tile = pl.BlockSpec((part, keys), lambda c: (c, 0))
+        return pl.pallas_call(
+            last_product,
+            grid=(nview,),
+            out_shape=(
+                jax.ShapeDtypeStruct(view_maps.shape, F32),
+                jax.ShapeDtypeStruct(shared.shape, F32),
+            ),
+            in_specs=[whole, tile, pl.BlockSpec((keys, keys), lambda c: (0, 0))],
+            out_specs=(whole, tile),
+        )(maps, average.reshape(rows, keys), root)
 
     in_specs = (P("view", "row", None), P("view", "row", None), P("row", None))
     out_specs = (P("view", "row", None), P("row", None))

time: 226 us -> 219 us (0.969)
  local copies, waits for them, and re-layouts: 4.71 us -> 0 us
    unnamed x2 -> x0, local copies, waits for them, and re-layouts: 4.71 us -> none
    pallas_call x1 -> x2, Pallas kernels: 220 us -> 218 us  [the longest x1 214 us: local(): pl.pallas_call(functools.partial(kernel, (nz, nx, ny, nc), pieces), out_s...]
where the time goes in v3:
time: 219 us
  Pallas kernels  218 us (100%)
    pallas_call x1, Pallas kernels, local(): pl.pallas_call(functools.partial(kernel, (nz, nx, ny, nc), pieces), out_s...  214 us
    pallas_call x1, Pallas kernels, local(): pl.pallas_call(last_product, grid=(nview,), out_shape=(jax.ShapeDtypeStru...  4.63 us

profile of v3, /device:TPU:24, one launch (start us, length us, event | category | flops | bytes accessed | tf_op | source)
XLA Modules:
  0.0 218.8 jit_solution(15739718172356785315)
XLA Ops:
  0.6 213.5 %shard_map.50 = (f32[1,256,256]{2,1,0:T(8,128)}, f32[4,512,256]{2,1,0:T(8,128)}, f32[256,256]{1,0:T(8,128)}) custom-call(f32[1,2048,2048]{2,1,0:T(8,128)} %f_ref.1, f32[1,256,256]{2,1,0:T(8,128)} %w_ref.1, f32[2048,256]{1,0:T(8,128)} %s_hbm.1), custom_call_target="tpu_custom_call" | custom-call | tf_op jit(solution)/shard_map/pallas_call | solution.py:643
  214.1 4.6 %shard_map.51 = (f32[1,256,256]{2,1,0:T(8,128)}, f32[2048,256]{1,0:T(8,128)}) custom-call(f32[1,256,256]{2,1,0:T(8,128)} %get-tuple-element.5.w_ref, f32[2048,256]{1,0:T(8,128)} %bitcast.1, f32[256,256]{1,0:T(8,128)} %get-tuple-element.7.root_ref), custom_call_target="tpu_custom_call" | custom-call | tf_op jit(solution)/shard_map/pallas_call | solution.py:681

commit v4 on v3

--- a/solution.py
+++ b/solution.py
@@ -14,6 +14,7 @@
 CORES = 2
 HALVES = 2
 CUT = 2
+LAST = 2
 MESH = pl.DeviceIdType.MESH
 F32 = jnp.float32
 BF16 = jnp.bfloat16
@@ -76,7 +77,8 @@
     chunk = fbuf.shape[1]
     nchunk = local // chunk
     part = local // nview
-    gpart = keys // nrow
+    side = keys // 2
+    gpart = side // nrow
     cut = len(pieces)
     rows_of = [pl.ds(a, n) for a, n in pieces]
     sub = 512
@@ -409,7 +411,9 @@
         own = av[it, view]
         hi, lo = split(own)
         thi, tlo = split(own.T)
-        gram[it] = dot3s((thi, tlo), (hi, lo)).reshape(nrow, gpart, keys)
+        full = dot3s((thi, tlo), (hi, lo))
+        upper = jnp.concatenate([full[:side], full[side:, side:]], axis=1)
+        gram[it] = upper.reshape(nrow, gpart, keys + side)
         for d in range(1, nrow):
             to = lax.rem(row + d, nrow)
             send(
@@ -451,7 +455,9 @@
         for d in range(1, nrow):
             src = lax.rem(row - d + nrow, nrow)
             recv(gfull.at[it, src], g3_s.at[d - 1], g3_r.at[d - 1], {"row": src})
-        return newton_steps(gfull[it].reshape(keys, keys))
+        upper = gfull[it].reshape(side, keys + side)
+        lower = jnp.concatenate([upper[:, side:keys].T, upper[:, keys:]], axis=1)
+        return newton_steps(jnp.concatenate([upper[:, :keys], lower], axis=0))
 
     def forward_average(it, h):
         for dy in range(1, ny):
@@ -537,32 +543,34 @@
     with ns("q_fa"):
         for h in range(HALVES - 1):
             forward_average(0, h)
-    with ns("q_g2"):
-        gram_views(0)
     with ns("q_fa"):
         forward_average(0, HALVES - 1)
-    with ns("q_g3"):
-        gram_rows(0)
     with ns("q_fin"):
         finish_average(0)
         ag_flush(1)
         for v in range(nview):
             put_rt(slice(v * part, (v + 1) * part), av[0, v])
+    with ns("q_g2"):
+        gram_views(0)
     with ns("q_rs2c"):
-        rs_compute(2)
+        rs_first(2, 0)
+    with ns("q_g3"):
+        gram_rows(0)
+    with ns("q_rs2c"):
+        rs_compute(2, 1)
     with ns("q_rs1o"):
         for p in range(cut):
             rs_own(1, p)
     with ns("q_rs2e"):
-        rs_event(2, far)
-    with ns("q_nw"):
-        steps = gram_end(0)
-        next(steps)
-        root, frob = next(steps)
-    with ns("q_rs2e"):
-        for i in range(1, nz - 1):
+        steps = None
+        for i in range(nz - 1):
             rs_event(2, far - i)
-            root, frob = next(steps, (root, frob))
+            if steps is None and i >= min(1, far):
+                with ns("q_nw"):
+                    steps = gram_end(0)
+                    root, frob = next(steps)
+            if steps is not None:
+                root, frob = next(steps, (root, frob))
         for root, frob in steps:
             pass
         rootc = split(root.T)
@@ -626,7 +634,8 @@
     def local(features, view_maps, shared):
         rows, width = features.shape[1], features.shape[2]
         shard, keys = view_maps.shape[1], view_maps.shape[2]
-        part, gpart = rows // nview, keys // nrow
+        part, side = rows // nview, keys // 2
+        gpart = side // nrow
         cut = CUT
         pieces = [(p * keys // cut, keys // cut) for p in range(cut)]
         chunk = 256
@@ -666,10 +675,10 @@
                 pltpu.VMEM((ITERS, ny, nc - 1, part, keys), F32),
                 pltpu.VMEM((ITERS, ny, part, keys), F32),
                 pltpu.VMEM((ITERS, nview, part, keys), F32),
-                pltpu.VMEM((ITERS, nrow, gpart, keys), F32),
-                pltpu.VMEM((ITERS, nrow, gpart, keys), F32),
-                pltpu.VMEM((ITERS, nview, gpart, keys), F32),
-                pltpu.VMEM((ITERS, nrow, gpart, keys), F32),
+                pltpu.VMEM((ITERS, nrow, gpart, keys + side), F32),
+                pltpu.VMEM((ITERS, nrow, gpart, keys + side), F32),
+                pltpu.VMEM((ITERS, nview, gpart, keys + side), F32),
+                pltpu.VMEM((ITERS, nrow, gpart, keys + side), F32),
                 dma((2,)), dma, dma,
             ] + sems,
             compiler_params=pltpu.CompilerParams(
@@ -677,10 +686,11 @@
             ),
         )(features, view_maps, shared)
         whole = pl.BlockSpec((1, shard, keys), lambda c: (0, 0, 0))
-        tile = pl.BlockSpec((part, keys), lambda c: (c, 0))
+        span = rows // LAST
+        tile = pl.BlockSpec((span, keys), lambda c: (c, 0))
         return pl.pallas_call(
             last_product,
-            grid=(nview,),
+            grid=(LAST,),
             out_shape=(
                 jax.ShapeDtypeStruct(view_maps.shape, F32),
                 jax.ShapeDtypeStruct(shared.shape, F32),

time: 219 us -> 216 us (0.986)
  Pallas kernels: 218 us -> 215 us
    pallas_call x1, Pallas kernels: 214 us -> 211 us  [local(): pl.pallas_call(functools.partial(kernel, (nz, nx, ny, nc), pieces), out_s...]
where the time goes in v4:
time: 216 us; the launch traced here: 215 us
  Pallas kernels  215 us (100%)
    pallas_call x1, Pallas kernels, local(): pl.pallas_call(functools.partial(kernel, (nz, nx, ny, nc), pieces), out_s...  211 us

profile of v4, /device:TPU:24, one launch (start us, length us, event | category | flops | bytes accessed | tf_op | source)
XLA Modules:
  0.0 215.1 jit_solution(2045282738259723946)
XLA Ops:
  0.6 211.0 %shard_map.50 = (f32[1,256,256]{2,1,0:T(8,128)}, f32[4,512,256]{2,1,0:T(8,128)}, f32[256,256]{1,0:T(8,128)}) custom-call(f32[1,2048,2048]{2,1,0:T(8,128)} %f_ref.1, f32[1,256,256]{2,1,0:T(8,128)} %w_ref.1, f32[2048,256]{1,0:T(8,128)} %s_hbm.1), custom_call_target="tpu_custom_call" | custom-call | tf_op jit(solution)/shard_map/pallas_call | solution.py:652
  211.6 3.5 %shard_map.51 = (f32[1,256,256]{2,1,0:T(8,128)}, f32[2048,256]{1,0:T(8,128)}) custom-call(f32[1,256,256]{2,1,0:T(8,128)} %get-tuple-element.5.w_ref, f32[2048,256]{1,0:T(8,128)} %bitcast.1, f32[256,256]{1,0:T(8,128)} %get-tuple-element.7.root_ref), custom_call_target="tpu_custom_call" | custom-call | tf_op jit(solution)/shard_map/pallas_call | solution.py:691
